TPU v7x, 32 devices: a whole 2x2x4 slice. The times are simulated.
32 devices in a mesh: gx: 4 (over z), gy: 8 (over y, x, core).
Axes of the slice: x: 2, y: 2, z: 4, core: 2. Of those that a mesh axis runs over, the one named last changes fastest.
Arguments:
- right_side: float32 [32, 128, 128], P('gx', 'gy'), may hold values from -8 to 8
- diagonal: float32 [32, 128, 128], P('gx', 'gy'), may hold values from 0.25 to 2
- solid_mask: int32 [32, 128, 128], P('gx', 'gy'), may hold values 0 or 1
- geneo_vectors: bfloat16 [32, 32, 128, 128], P(None, 'gx', 'gy'), may hold values from -0.046875 to 0.046875
- vector_counts: int32 [4, 8], P('gx', 'gy'), may hold values from 8 to 32, as said below
- owner_slots: int32 [32], replicated, may hold values from 0 to 31, each once
- coarse_inverse: float32 [1024, 64], P('gy'), may hold values from -1 to 8, as said below
Outputs:
- solution: float32 [32, 128, 128], P('gx', 'gy')
- residual: float32 [32, 128, 128], P('gx', 'gy')
Inputs may be any that keep to these rules, and one draw needn't show every extreme that they name: `vector_counts`: every count lies between 8 and 32; both ends occur in every draw. Subdomain s belongs to coarse block owner_slots[s] // 2. `coarse_inverse`: each block is symmetric positive definite; rows and columns beyond a subdomain's count are unused.
All inputs are finite; a program needn't handle non-finite values. No bound on the sum of `solid_mask` on one device may be relied on, other than what follows from the above.
Results may differ from a plain program's by a relative error of at most 0.0003.
Values sent between devices are 32-bit elements; how exact they have to be, the bound alone decides.
No kernel may reach another device: no remote copies, remote signals or barrier semaphores. Data moves between devices by JAX's collectives and lax.ppermute only.
A program may use at most 64 MiB of HBM per device.

v0:
```python
import jax
import jax.numpy as jnp
from jax import lax
from jax.sharding import PartitionSpec as P

DEG = 3
ITERS = 2


CHEB_LO = 0.3
CHEB_HI = 2.0
HIGH = lax.Precision.HIGHEST


def with_halo(cells, sides, width):
    for axis, dim in sides:
        count = lax.axis_size(axis)
        ends = count - 1
        head = lax.slice_in_dim(cells, 0, width, axis=dim)
        tail = lax.slice_in_dim(cells, cells.shape[dim] - width, cells.shape[dim], axis=dim)
        cells = jnp.concatenate(
            [
                lax.ppermute(tail, axis, [(i, (i + 1) % count) for i in range(ends)]),
                cells,
                lax.ppermute(head, axis, [((i + 1) % count, i) for i in range(ends)]),
            ],
            axis=dim,
        )
    return cells


def operate(field, diagonal, fluid):
    masked = fluid * field
    padded = with_halo(masked, (("gx", 0), ("gy", 1)), 1)
    beside = padded[2:, 1:-1] + padded[:-2, 1:-1] + padded[1:-1, 2:] + padded[1:-1, :-2]
    vertical = jnp.pad(masked, ((0, 0), (0, 0), (1, 1)))
    beside = beside + vertical[:, :, 2:] + vertical[:, :, :-2]
    return fluid * ((6.0 + diagonal) * field - beside) + (1.0 - fluid) * field


def smoother(res, diagonal, fluid, jacobi):
    centre = (CHEB_HI + CHEB_LO) / 2.0
    half_width = (CHEB_HI - CHEB_LO) / 2.0
    sigma_val = centre / half_width
    rho_old = 1.0 / sigma_val
    update = jacobi * res / centre
    smooth = update
    remainder = res
    for repeat in range(DEG - 1):
        remainder = remainder - operate(update, diagonal, fluid)
        rho_new = 1.0 / (2.0 * sigma_val - rho_old)
        update = rho_new * rho_old * update + 2.0 * rho_new / half_width * jacobi * remainder
        smooth = smooth + update
        rho_old = rho_new
    return smooth


def on_device(
    right_side, diagonal, solid_mask, geneo_vectors, vector_counts, owner_slots, coarse_inverse
):
    fluid = 1.0 - solid_mask.astype(jnp.float32)
    jacobi = 1.0 / (fluid * (6.0 + diagonal) + 1.0 - fluid)
    kcount = geneo_vectors.shape[0]
    shape_cells = right_side.shape
    live = (jnp.arange(kcount, dtype=jnp.int32) < vector_counts[0, 0]).astype(jnp.float32)
    vec_matrix = geneo_vectors.reshape(kcount, -1).astype(jnp.float32) * live[:, None]
    row_count = coarse_inverse.shape[0]
    block_len = coarse_inverse.shape[1]
    size_gy = lax.axis_size("gy")
    index_gx = lax.axis_index("gx")
    index_gy = lax.axis_index("gy")
    my_sub = index_gx * size_gy + index_gy
    my_slot = lax.dynamic_slice_in_dim(owner_slots, my_sub, 1, 0)[0]

    def precondition(res):
        smooth = smoother(res, diagonal, fluid, jacobi)
        projected = jnp.dot(vec_matrix, res.reshape(-1), precision=HIGH)
        every_rhs = lax.all_gather(projected[None, :], ("gx", "gy"), axis=0, tiled=True)
        ordered = jnp.zeros(every_rhs.shape, jnp.float32).at[owner_slots].set(every_rhs)
        ordered_blocks = ordered.reshape(-1, block_len)
        first_row = index_gy * row_count
        row_ids = first_row + jnp.arange(row_count, dtype=jnp.int32)
        picked = ordered_blocks[row_ids // block_len]
        coarse_part = jnp.sum(coarse_inverse * picked, axis=1)
        coarse_full = lax.all_gather(coarse_part, "gy", axis=0, tiled=True)
        coeffs = lax.dynamic_slice_in_dim(coarse_full.reshape(-1, kcount), my_slot, 1, 0)[0] * live
        fine = jnp.dot(coeffs, vec_matrix, precision=HIGH)
        inner = None
        return (smooth + fine.reshape(shape_cells), inner)

    def products(resid, pre, pre_image):
        return lax.psum((jnp.sum(resid * pre), jnp.sum(pre * pre_image)), ("gx", "gy"))

    solution = jnp.zeros_like(right_side)
    residual = right_side
    precond, inner = precondition(residual)
    image_pre = operate(precond, diagonal, fluid)
    norm_now, curvature = products(residual, precond, image_pre)
    step_len = norm_now / curvature
    direction = precond
    along = image_pre
    for repeat in range(ITERS):
        solution = solution + step_len * direction
        residual = residual - step_len * along
        if repeat + 1 < ITERS:
            precond, inner = precondition(residual)
            image_pre = operate(precond, diagonal, fluid)
            norm_next, curvature = products(residual, precond, image_pre)
            ratio_val = norm_next / norm_now
            step_len = norm_next / (curvature - ratio_val * norm_next / step_len)
            direction = precond + ratio_val * direction
            along = image_pre + ratio_val * along
            norm_now = norm_next
    return (solution, residual)


def solution(mesh):
    in_specs = (
        P("gx", "gy", None),
        P("gx", "gy", None),
        P("gx", "gy", None),
        P(None, "gx", "gy", None),
        P("gx", "gy"),
        P(),
        P("gy", None),
    )
    out_specs = (P("gx", "gy", None), P("gx", "gy", None))
    return jax.shard_map(
        on_device, mesh=mesh, in_specs=in_specs, out_specs=out_specs, check_vma=False
    )
```

profile of v0, /device:TPU:0, one launch (start us, length us, event | category | flops | bytes accessed | tf_op | source)
XLA Modules:
  0.0 304.8 jit_solution(2894546075494403240)
XLA Ops:
  3.0 5.6 %collective-permute-start.1 = (f32[1,16,128]{2,1,0:T(8,128)S(1)}, f32[1,16,128]{2,1,0:T(8,128)S(1)}, u32[]{:S(2)}, u32[]{:S(2)}) collective-permute-start(f32[1,16,128]{2,1,0:T(8,128)S(1)} %get-tuple-element.40), channel_id=1, source_target_pairs={{0,8},{8,16},{16,24},{1,9},{9,17},{17,25},{2,10},{10,18},{18,26},{... | collective-permute-start | bytes 24584 | tf_op jit(solution)/shard_map/ppermute | solution.py:23
  10.9 2.5 fusion
  13.5 2.8 fusion.9
  19.5 43.7 %all-reduce.6 = f32[1024]{0:T(1024)S(1)} all-reduce(f32[1024]{0:T(1024)S(1)} %dynamic-update-slice), channel_id=2, replica_groups=mesh['gx'=4,'gy'=8] {'gx','gy'}, use_global_device_ids=true, to_apply=%add.6 | all-reduce | flops 1024 | bytes 8192
  66.1 4.5 %collective-permute-start.5 = (f32[1,16,128]{2,1,0:T(8,128)S(1)}, f32[1,16,128]{2,1,0:T(8,128)S(1)}, u32[]{:S(2)}, u32[]{:S(2)}) collective-permute-start(f32[1,16,128]{2,1,0:T(8,128)S(1)} %get-tuple-element.38), channel_id=1, source_target_pairs={{0,8},{8,16},{16,24},{1,9},{9,17},{17,25},{2,10},{10,18},{18,26},{... | collective-permute-start | bytes 24584 | tf_op jit(solution)/shard_map/ppermute | solution.py:23
  72.8 3.3 %copy.24 = f32[4,8,128,128]{3,2,1,0:T(8,128)} copy(f32[4,8,128,128]{3,1,2,0:T(8,128)} %fusion) | data formatting | bytes 4194304
  76.1 9.5 %all-gather.2 = f32[8,1,128]{2,1,0:T(1,128)S(1)} all-gather(f32[1,1,128]{2,1,0:T(1,128)S(1)} %bitcast.64), channel_id=1, replica_groups=mesh['gx'=4,'gy'=8] {'gy'}, dimensions={0}, use_global_device_ids=true | all-gather | bytes 4608 | tf_op jit(solution)/shard_map/all_gather | solution.py:85
  87.6 2.2 collective-permute-start.7
  91.1 3.8 %fusion.3 = f32[1,8,16,128]{3,0,2,1:T(1,128)S(1)} fusion(f32[8,16,128,32]{2,1,0,3:T(8,128)} %bitcast.57, f32[32,32]{1,0:T(8,128)S(1)} %reshape.114, s32[]{:T(128)S(6)} %select_n.39, s32[]{:T(128)} %bitcast.54), kind=kOutput, calls=%fused_computation.8 | convolution fusion | flops 6291520 | bytes 2163208 | tf_op jit(solution)/shard_map/dot_general | solution.py:87
  96.4 4.5 %collective-permute-start.9 = (f32[1,16,128]{2,1,0:T(8,128)S(1)}, f32[1,16,128]{2,1,0:T(8,128)S(1)}, u32[]{:S(2)}, u32[]{:S(2)}) collective-permute-start(f32[1,16,128]{2,1,0:T(8,128)S(1)} %get-tuple-element.36), channel_id=1, source_target_pairs={{0,8},{8,16},{16,24},{1,9},{9,17},{17,25},{2,10},{10,18},{18,26},{... | collective-permute-start | bytes 24584 | tf_op jit(solution)/shard_map/ppermute | solution.py:23
  102.4 2.6 collective-permute-start.11
  106.3 4.1 %collective-permute-done.10 = f32[10,1,128]{2,1,0:T(1,128)S(1)} collective-permute-done((f32[10,1,128]{2,1,0:T(1,128)S(1)}, f32[10,1,128]{2,1,0:T(1,128)S(1)}, u32[]{:S(2)}, u32[]{:S(2)}) %collective-permute-start.10) | collective-permute-done | bytes 5152 | tf_op jit(solution)/shard_map/ppermute | solution.py:25
  111.2 43.8 %all-reduce.9 = (f32[]{:T(128)}, f32[]{:T(128)}) all-reduce(f32[]{:T(128)} %get-tuple-element.5, f32[]{:T(128)} %get-tuple-element.4), channel_id=1, replica_groups=mesh['gx'=4,'gy'=8] {'gx','gy'}, use_global_device_ids=true, to_apply=%region_3.4 | all-reduce | flops 2 | bytes 16 | tf_op jit(solution)/shard_map/psum | solution.py:92
  157.7 4.5 %collective-permute-start.13 = (f32[1,16,128]{2,1,0:T(8,128)S(1)}, f32[1,16,128]{2,1,0:T(8,128)S(1)}, u32[]{:S(2)}, u32[]{:S(2)}) collective-permute-start(f32[1,16,128]{2,1,0:T(8,128)S(1)} %get-tuple-element.34), channel_id=1, source_target_pairs={{0,8},{8,16},{16,24},{1,9},{9,17},{17,25},{2,10},{10,18},{18,26},{... | collective-permute-start | bytes 24584 | tf_op jit(solution)/shard_map/ppermute | solution.py:23
  166.4 2.8 fusion.12
  169.3 44.4 %all-reduce.7 = f32[1024]{0:T(1024)S(1)} all-reduce(f32[1024]{0:T(1024)S(1)} %dynamic-update-slice.1), channel_id=3, replica_groups=mesh['gx'=4,'gy'=8] {'gx','gy'}, use_global_device_ids=true, to_apply=%add.7 | all-reduce | flops 1024 | bytes 8192
  216.7 4.5 %collective-permute-start.17 = (f32[1,16,128]{2,1,0:T(8,128)S(1)}, f32[1,16,128]{2,1,0:T(8,128)S(1)}, u32[]{:S(2)}, u32[]{:S(2)}) collective-permute-start(f32[1,16,128]{2,1,0:T(8,128)S(1)} %get-tuple-element.32), channel_id=1, source_target_pairs={{0,8},{8,16},{16,24},{1,9},{9,17},{17,25},{2,10},{10,18},{18,26},{... | collective-permute-start | bytes 24584 | tf_op jit(solution)/shard_map/ppermute | solution.py:23
  221.3 9.6 %all-gather.3 = f32[8,1,128]{2,1,0:T(1,128)S(1)} all-gather(f32[1,1,128]{2,1,0:T(1,128)S(1)} %bitcast.65), channel_id=1, replica_groups=mesh['gx'=4,'gy'=8] {'gy'}, dimensions={0}, use_global_device_ids=true | all-gather | bytes 4608 | tf_op jit(solution)/shard_map/all_gather | solution.py:85
  231.6 2.2 collective-permute-start.19
  235.2 3.8 %fusion.1 = f32[1,8,16,128]{3,0,2,1:T(1,128)S(1)} fusion(f32[8,16,128,32]{2,1,0,3:T(8,128)} %bitcast.58, f32[32,32]{1,0:T(8,128)S(1)} %reshape.116, s32[]{:T(128)S(6)} %select_n.39, s32[]{:T(128)} %bitcast.56), kind=kOutput, calls=%fused_computation.6 | convolution fusion | flops 6291520 | bytes 2163208 | tf_op jit(solution)/shard_map/dot_general | solution.py:87
  240.5 4.5 %collective-permute-start.21 = (f32[1,16,128]{2,1,0:T(8,128)S(1)}, f32[1,16,128]{2,1,0:T(8,128)S(1)}, u32[]{:S(2)}, u32[]{:S(2)}) collective-permute-start(f32[1,16,128]{2,1,0:T(8,128)S(1)} %get-tuple-element.30), channel_id=1, source_target_pairs={{0,8},{8,16},{16,24},{1,9},{9,17},{17,25},{2,10},{10,18},{18,26},{... | collective-permute-start | bytes 24584 | tf_op jit(solution)/shard_map/ppermute | solution.py:23
  246.4 3.1 %collective-permute-start.23 = (f32[10,1,128]{2,1,0:T(1,128)S(1)}, f32[10,1,128]{2,1,0:T(1,128)S(1)}, u32[]{:S(2)}, u32[]{:S(2)}) collective-permute-start(f32[10,1,128]{2,1,0:T(1,128)S(1)} %get-tuple-element.19), channel_id=1, source_target_pairs={{0,1},{1,2},{2,3},{3,4},{4,5},{5,6},{6,7},{8,9},{9,10},{10,11},{11... | collective-permute-start | bytes 15368 | tf_op jit(solution)/shard_map/ppermute | solution.py:23
  250.8 4.1 %collective-permute-done.22 = f32[10,1,128]{2,1,0:T(1,128)S(1)} collective-permute-done((f32[10,1,128]{2,1,0:T(1,128)S(1)}, f32[10,1,128]{2,1,0:T(1,128)S(1)}, u32[]{:S(2)}, u32[]{:S(2)}) %collective-permute-start.22) | collective-permute-done | bytes 5152 | tf_op jit(solution)/shard_map/ppermute | solution.py:25
  255.7 43.8 %all-reduce.8 = (f32[]{:T(128)}, f32[]{:T(128)}) all-reduce(f32[]{:T(128)} %get-tuple-element.3, f32[]{:T(128)} %get-tuple-element.2), channel_id=1, replica_groups=mesh['gx'=4,'gy'=8] {'gx','gy'}, use_global_device_ids=true, to_apply=%region_9.10 | all-reduce | flops 2 | bytes 16 | tf_op jit(solution)/shard_map/psum | solution.py:92
  (96 shorter events, 34.4 us)
Async XLA Ops:
  1.7 14.6 %collective-permute-start = (f32[1,16,128]{2,1,0:T(8,128)S(1)}, f32[1,16,128]{2,1,0:T(8,128)S(1)}, u32[]{:S(2)}, u32[]{:S(2)}) collective-permute-start(f32[1,16,128]{2,1,0:T(8,128)S(1)} %get-tuple-element.41), channel_id=1, source_target_pairs={{8,0},{16,8},{24,16},{9,1},{17,9},{25,17},{10,2},{18,10},{26,18},{... | collective-permute-start | bytes 24584 | tf_op jit(solution)/shard_map/ppermute | solution.py:25
  3.0 13.3 %collective-permute-start.1 = (f32[1,16,128]{2,1,0:T(8,128)S(1)}, f32[1,16,128]{2,1,0:T(8,128)S(1)}, u32[]{:S(2)}, u32[]{:S(2)}) collective-permute-start(f32[1,16,128]{2,1,0:T(8,128)S(1)} %get-tuple-element.40), channel_id=1, source_target_pairs={{0,8},{8,16},{16,24},{1,9},{9,17},{17,25},{2,10},{10,18},{18,26},{... | collective-permute-start | bytes 24584 | tf_op jit(solution)/shard_map/ppermute | solution.py:23
  16.3 48.3 %collective-permute-start.3 = (f32[10,1,128]{2,1,0:T(1,128)S(1)}, f32[10,1,128]{2,1,0:T(1,128)S(1)}, u32[]{:S(2)}, u32[]{:S(2)}) collective-permute-start(f32[10,1,128]{2,1,0:T(1,128)S(1)} %get-tuple-element.29), channel_id=1, source_target_pairs={{0,1},{1,2},{2,3},{3,4},{4,5},{5,6},{6,7},{8,9},{9,10},{10,11},{11... | collective-permute-start | bytes 15368 | tf_op jit(solution)/shard_map/ppermute | solution.py:23
  17.8 46.8 %collective-permute-start.2 = (f32[10,1,128]{2,1,0:T(1,128)S(1)}, f32[10,1,128]{2,1,0:T(1,128)S(1)}, u32[]{:S(2)}, u32[]{:S(2)}) collective-permute-start(f32[10,1,128]{2,1,0:T(1,128)S(1)} %get-tuple-element.28), channel_id=1, source_target_pairs={{1,0},{2,1},{3,2},{4,3},{5,4},{6,5},{7,6},{9,8},{10,9},{11,10},{12... | collective-permute-start | bytes 15368 | tf_op jit(solution)/shard_map/ppermute | solution.py:25
  64.8 22.7 %collective-permute-start.4 = (f32[1,16,128]{2,1,0:T(8,128)S(1)}, f32[1,16,128]{2,1,0:T(8,128)S(1)}, u32[]{:S(2)}, u32[]{:S(2)}) collective-permute-start(f32[1,16,128]{2,1,0:T(8,128)S(1)} %get-tuple-element.39), channel_id=1, source_target_pairs={{8,0},{16,8},{24,16},{9,1},{17,9},{25,17},{10,2},{18,10},{26,18},{... | collective-permute-start | bytes 24584 | tf_op jit(solution)/shard_map/ppermute | solution.py:25
  66.1 21.5 %collective-permute-start.5 = (f32[1,16,128]{2,1,0:T(8,128)S(1)}, f32[1,16,128]{2,1,0:T(8,128)S(1)}, u32[]{:S(2)}, u32[]{:S(2)}) collective-permute-start(f32[1,16,128]{2,1,0:T(8,128)S(1)} %get-tuple-element.38), channel_id=1, source_target_pairs={{0,8},{8,16},{16,24},{1,9},{9,17},{17,25},{2,10},{10,18},{18,26},{... | collective-permute-start | bytes 24584 | tf_op jit(solution)/shard_map/ppermute | solution.py:23
  87.6 7.3 %collective-permute-start.7 = (f32[10,1,128]{2,1,0:T(1,128)S(1)}, f32[10,1,128]{2,1,0:T(1,128)S(1)}, u32[]{:S(2)}, u32[]{:S(2)}) collective-permute-start(f32[10,1,128]{2,1,0:T(1,128)S(1)} %get-tuple-element.27), channel_id=1, source_target_pairs={{0,1},{1,2},{2,3},{3,4},{4,5},{5,6},{6,7},{8,9},{9,10},{10,11},{11... | collective-permute-start | bytes 15368 | tf_op jit(solution)/shard_map/ppermute | solution.py:23
  89.8 5.1 %collective-permute-start.6 = (f32[10,1,128]{2,1,0:T(1,128)S(1)}, f32[10,1,128]{2,1,0:T(1,128)S(1)}, u32[]{:S(2)}, u32[]{:S(2)}) collective-permute-start(f32[10,1,128]{2,1,0:T(1,128)S(1)} %get-tuple-element.26), channel_id=1, source_target_pairs={{1,0},{2,1},{3,2},{4,3},{5,4},{6,5},{7,6},{9,8},{10,9},{11,10},{12... | collective-permute-start | bytes 15368 | tf_op jit(solution)/shard_map/ppermute | solution.py:25
  95.1 5.9 %collective-permute-start.8 = (f32[1,16,128]{2,1,0:T(8,128)S(1)}, f32[1,16,128]{2,1,0:T(8,128)S(1)}, u32[]{:S(2)}, u32[]{:S(2)}) collective-permute-start(f32[1,16,128]{2,1,0:T(8,128)S(1)} %get-tuple-element.37), channel_id=1, source_target_pairs={{8,0},{16,8},{24,16},{9,1},{17,9},{25,17},{10,2},{18,10},{26,18},{... | collective-permute-start | bytes 24584 | tf_op jit(solution)/shard_map/ppermute | solution.py:25
  96.4 5.9 %collective-permute-start.9 = (f32[1,16,128]{2,1,0:T(8,128)S(1)}, f32[1,16,128]{2,1,0:T(8,128)S(1)}, u32[]{:S(2)}, u32[]{:S(2)}) collective-permute-start(f32[1,16,128]{2,1,0:T(8,128)S(1)} %get-tuple-element.36), channel_id=1, source_target_pairs={{0,8},{8,16},{16,24},{1,9},{9,17},{17,25},{2,10},{10,18},{18,26},{... | collective-permute-start | bytes 24584 | tf_op jit(solution)/shard_map/ppermute | solution.py:23
  102.4 3.9 %collective-permute-start.11 = (f32[10,1,128]{2,1,0:T(1,128)S(1)}, f32[10,1,128]{2,1,0:T(1,128)S(1)}, u32[]{:S(2)}, u32[]{:S(2)}) collective-permute-start(f32[10,1,128]{2,1,0:T(1,128)S(1)} %get-tuple-element.25), channel_id=1, source_target_pairs={{0,1},{1,2},{2,3},{3,4},{4,5},{5,6},{6,7},{8,9},{9,10},{10,11},{11... | collective-permute-start | bytes 15368 | tf_op jit(solution)/shard_map/ppermute | solution.py:23
  105.0 5.4 %collective-permute-start.10 = (f32[10,1,128]{2,1,0:T(1,128)S(1)}, f32[10,1,128]{2,1,0:T(1,128)S(1)}, u32[]{:S(2)}, u32[]{:S(2)}) collective-permute-start(f32[10,1,128]{2,1,0:T(1,128)S(1)} %get-tuple-element.24), channel_id=1, source_target_pairs={{1,0},{2,1},{3,2},{4,3},{5,4},{6,5},{7,6},{9,8},{10,9},{11,10},{12... | collective-permute-start | bytes 15368 | tf_op jit(solution)/shard_map/ppermute | solution.py:25
  156.4 5.9 %collective-permute-start.12 = (f32[1,16,128]{2,1,0:T(8,128)S(1)}, f32[1,16,128]{2,1,0:T(8,128)S(1)}, u32[]{:S(2)}, u32[]{:S(2)}) collective-permute-start(f32[1,16,128]{2,1,0:T(8,128)S(1)} %get-tuple-element.35), channel_id=1, source_target_pairs={{8,0},{16,8},{24,16},{9,1},{17,9},{25,17},{10,2},{18,10},{26,18},{... | collective-permute-start | bytes 24584 | tf_op jit(solution)/shard_map/ppermute | solution.py:25
  157.7 5.9 %collective-permute-start.13 = (f32[1,16,128]{2,1,0:T(8,128)S(1)}, f32[1,16,128]{2,1,0:T(8,128)S(1)}, u32[]{:S(2)}, u32[]{:S(2)}) collective-permute-start(f32[1,16,128]{2,1,0:T(8,128)S(1)} %get-tuple-element.34), channel_id=1, source_target_pairs={{0,8},{8,16},{16,24},{1,9},{9,17},{17,25},{2,10},{10,18},{18,26},{... | collective-permute-start | bytes 24584 | tf_op jit(solution)/shard_map/ppermute | solution.py:23
  163.6 51.6 %collective-permute-start.15 = (f32[10,1,128]{2,1,0:T(1,128)S(1)}, f32[10,1,128]{2,1,0:T(1,128)S(1)}, u32[]{:S(2)}, u32[]{:S(2)}) collective-permute-start(f32[10,1,128]{2,1,0:T(1,128)S(1)} %get-tuple-element.23), channel_id=1, source_target_pairs={{0,1},{1,2},{2,3},{3,4},{4,5},{5,6},{6,7},{8,9},{9,10},{10,11},{11... | collective-permute-start | bytes 15368 | tf_op jit(solution)/shard_map/ppermute | solution.py:23
  164.9 50.3 %collective-permute-start.14 = (f32[10,1,128]{2,1,0:T(1,128)S(1)}, f32[10,1,128]{2,1,0:T(1,128)S(1)}, u32[]{:S(2)}, u32[]{:S(2)}) collective-permute-start(f32[10,1,128]{2,1,0:T(1,128)S(1)} %get-tuple-element.22), channel_id=1, source_target_pairs={{1,0},{2,1},{3,2},{4,3},{5,4},{6,5},{7,6},{9,8},{10,9},{11,10},{12... | collective-permute-start | bytes 15368 | tf_op jit(solution)/shard_map/ppermute | solution.py:25
  215.4 16.3 %collective-permute-start.16 = (f32[1,16,128]{2,1,0:T(8,128)S(1)}, f32[1,16,128]{2,1,0:T(8,128)S(1)}, u32[]{:S(2)}, u32[]{:S(2)}) collective-permute-start(f32[1,16,128]{2,1,0:T(8,128)S(1)} %get-tuple-element.33), channel_id=1, source_target_pairs={{8,0},{16,8},{24,16},{9,1},{17,9},{25,17},{10,2},{18,10},{26,18},{... | collective-permute-start | bytes 24584 | tf_op jit(solution)/shard_map/ppermute | solution.py:25
  216.7 15.0 %collective-permute-start.17 = (f32[1,16,128]{2,1,0:T(8,128)S(1)}, f32[1,16,128]{2,1,0:T(8,128)S(1)}, u32[]{:S(2)}, u32[]{:S(2)}) collective-permute-start(f32[1,16,128]{2,1,0:T(8,128)S(1)} %get-tuple-element.32), channel_id=1, source_target_pairs={{0,8},{8,16},{16,24},{1,9},{9,17},{17,25},{2,10},{10,18},{18,26},{... | collective-permute-start | bytes 24584 | tf_op jit(solution)/shard_map/ppermute | solution.py:23
  231.6 7.3 %collective-permute-start.19 = (f32[10,1,128]{2,1,0:T(1,128)S(1)}, f32[10,1,128]{2,1,0:T(1,128)S(1)}, u32[]{:S(2)}, u32[]{:S(2)}) collective-permute-start(f32[10,1,128]{2,1,0:T(1,128)S(1)} %get-tuple-element.21), channel_id=1, source_target_pairs={{0,1},{1,2},{2,3},{3,4},{4,5},{5,6},{6,7},{8,9},{9,10},{10,11},{11... | collective-permute-start | bytes 15368 | tf_op jit(solution)/shard_map/ppermute | solution.py:23
  233.9 5.1 %collective-permute-start.18 = (f32[10,1,128]{2,1,0:T(1,128)S(1)}, f32[10,1,128]{2,1,0:T(1,128)S(1)}, u32[]{:S(2)}, u32[]{:S(2)}) collective-permute-start(f32[10,1,128]{2,1,0:T(1,128)S(1)} %get-tuple-element.20), channel_id=1, source_target_pairs={{1,0},{2,1},{3,2},{4,3},{5,4},{6,5},{7,6},{9,8},{10,9},{11,10},{12... | collective-permute-start | bytes 15368 | tf_op jit(solution)/shard_map/ppermute | solution.py:25
  239.2 5.9 %collective-permute-start.20 = (f32[1,16,128]{2,1,0:T(8,128)S(1)}, f32[1,16,128]{2,1,0:T(8,128)S(1)}, u32[]{:S(2)}, u32[]{:S(2)}) collective-permute-start(f32[1,16,128]{2,1,0:T(8,128)S(1)} %get-tuple-element.31), channel_id=1, source_target_pairs={{8,0},{16,8},{24,16},{9,1},{17,9},{25,17},{10,2},{18,10},{26,18},{... | collective-permute-start | bytes 24584 | tf_op jit(solution)/shard_map/ppermute | solution.py:25
  240.5 5.9 %collective-permute-start.21 = (f32[1,16,128]{2,1,0:T(8,128)S(1)}, f32[1,16,128]{2,1,0:T(8,128)S(1)}, u32[]{:S(2)}, u32[]{:S(2)}) collective-permute-start(f32[1,16,128]{2,1,0:T(8,128)S(1)} %get-tuple-element.30), channel_id=1, source_target_pairs={{0,8},{8,16},{16,24},{1,9},{9,17},{17,25},{2,10},{10,18},{18,26},{... | collective-permute-start | bytes 24584 | tf_op jit(solution)/shard_map/ppermute | solution.py:23
  246.4 4.4 %collective-permute-start.23 = (f32[10,1,128]{2,1,0:T(1,128)S(1)}, f32[10,1,128]{2,1,0:T(1,128)S(1)}, u32[]{:S(2)}, u32[]{:S(2)}) collective-permute-start(f32[10,1,128]{2,1,0:T(1,128)S(1)} %get-tuple-element.19), channel_id=1, source_target_pairs={{0,1},{1,2},{2,3},{3,4},{4,5},{5,6},{6,7},{8,9},{9,10},{10,11},{11... | collective-permute-start | bytes 15368 | tf_op jit(solution)/shard_map/ppermute | solution.py:23
  249.5 5.4 %collective-permute-start.22 = (f32[10,1,128]{2,1,0:T(1,128)S(1)}, f32[10,1,128]{2,1,0:T(1,128)S(1)}, u32[]{:S(2)}, u32[]{:S(2)}) collective-permute-start(f32[10,1,128]{2,1,0:T(1,128)S(1)} %get-tuple-element.18), channel_id=1, source_target_pairs={{1,0},{2,1},{3,2},{4,3},{5,4},{6,5},{7,6},{9,8},{10,9},{11,10},{12... | collective-permute-start | bytes 15368 | tf_op jit(solution)/shard_map/ppermute | solution.py:25
  (6 other events, 123.2 us)
where the time goes:
time: 306 us; the launch traced here: 305 us
  blocking collectives  195 us (64%)
  starting transfers between devices  57 us (19%)
  matrix products  13 us (4%)
  waiting for transfers between devices  12.3 us (4%)
  between operations  10 us (3%)
  other arithmetic  9.63 us (3%)
  local copies, waits for them, and re-layouts  8.08 us (3%)
    unnamed x2, blocking collectives  88.1 us
    psum x2, blocking collectives, products(): lax.psum((jnp.sum(resid * pre), jnp.sum(pre * pre_image)), ('gx', 'gy'))  87.5 us
    ppermute x12, starting transfers between devices, with_halo(): lax.ppermute(tail, axis, [(i, (i + 1) % count) for i in range(ends)])  41.3 us
    all_gather x2, blocking collectives, precondition(): coarse_full = lax.all_gather(coarse_part, 'gy', axis=0, tiled=True)  19.1 us
    ppermute x12, starting transfers between devices, with_halo(): lax.ppermute(head, axis, [((i + 1) % count, i) for i in range(ends)])  15.7 us
    ppermute x12, waiting for transfers between devices, with_halo(): lax.ppermute(head, axis, [((i + 1) % count, i) for i in range(ends)])  8.28 us
    dot_general x2, matrix products, precondition(): fine = jnp.dot(coeffs, vec_matrix, precision=HIGH)  7.52 us
  transfers between devices with their start and end apart: 24, of which 5 were waited for; matrix products, arithmetic and copies ran while one was open for 9% of the time, Pallas kernels for 0%

commit v1 on v0

v1 whole, which is shorter than its diff:
```python
import functools

import jax
import jax.numpy as jnp
from jax import lax
from jax.experimental import pallas as pl
from jax.experimental.pallas import tpu as pltpu
from jax.sharding import PartitionSpec as P

DEG = 3
CHEB_LO = 0.3
CHEB_HI = 2.0
H = 4
HR = 2
LANES = 128
VMEM = pl.BlockSpec(memory_space=pltpu.VMEM)
SMEM = pl.BlockSpec(memory_space=pltpu.SMEM)


def call(body, out, *args, scratch=(), smem=0):
    shapes = [jax.ShapeDtypeStruct(s, jnp.float32) for s in out]
    return pl.pallas_call(
        body,
        out_shape=shapes,
        in_specs=[SMEM] * smem + [VMEM] * (len(args) - smem),
        out_specs=[VMEM] * len(out),
        scratch_shapes=list(scratch),
    )(*args)


def beside(masked):
    rows, lanes = masked[0].shape
    lane = lax.broadcasted_iota(jnp.int32, (rows, lanes), 1)
    first, last = lane == 0, lane == lanes - 1
    out = []
    for i in range(1, len(masked) - 1):
        mid = masked[i]
        total = masked[i + 1] + masked[i - 1]
        total = total + pltpu.roll(mid, 1, 0) + pltpu.roll(mid, rows - 1, 0)
        total = total + jnp.where(first, 0.0, pltpu.roll(mid, 1, 1))
        total = total + jnp.where(last, 0.0, pltpu.roll(mid, lanes - 1, 1))
        out.append(total)
    return out


def operate(field, centre, fluid):
    near = beside([f * v for f, v in zip(fluid, field)])
    n = len(field)
    return [centre[i] * field[i] - fluid[i] * near[i - 1] for i in range(1, n - 1)]


def inner(rows, k):
    return rows[k:len(rows) - k] if k else rows


def smoother(res, centre, fluid, jacobi):
    theta = (CHEB_HI + CHEB_LO) / 2.0
    delta = (CHEB_HI - CHEB_LO) / 2.0
    sigma = theta / delta
    rho = 1.0 / sigma
    update = [j * r * (1.0 / theta) for j, r in zip(jacobi, res)]
    smooth = update
    rest = res
    for step in range(DEG - 1):
        image = operate(update, inner(centre, step), inner(fluid, step))
        rest = [a - b for a, b in zip(inner(rest, 1), image)]
        rho_new = 1.0 / (2.0 * sigma - rho)
        near_j = inner(jacobi, step + 1)
        update = [
            rho_new * rho * u + (2.0 * rho_new / delta) * (j * r)
            for u, j, r in zip(inner(update, 1), near_j, rest)
        ]
        smooth = [a + b for a, b in zip(inner(smooth, 1), update)]
        rho = rho_new
    return smooth


def total(rows):
    acc = rows[0]
    for r in rows[1:]:
        acc = acc + r
    return jnp.sum(jnp.sum(acc, axis=0, keepdims=True), axis=1, keepdims=True)


def lane_group(width):
    return lax.broadcasted_iota(jnp.int32, (1, LANES), 1) // width


def project(vec_ref, rows, count):
    kcount, nx = vec_ref.shape[:2]
    sums = []
    for k in range(kcount):
        acc = None
        for i in range(nx):
            term = vec_ref[k, i].astype(jnp.float32) * rows[i]
            acc = term if acc is None else acc + term
        sums.append(jnp.sum(acc, axis=0, keepdims=True))
    col = jnp.sum(jnp.concatenate(sums, axis=0), axis=1, keepdims=True)
    lane = lax.broadcasted_iota(jnp.int32, (kcount, LANES), 1)
    row = lax.broadcasted_iota(jnp.int32, (kcount, LANES), 0)
    picked = jnp.where((lane % kcount == row) & (row < count), col, 0.0)
    return jnp.sum(picked, axis=0, keepdims=True)


def prolong(vec_ref, coeffs):
    kcount, nx, ny, nz = vec_ref.shape
    rows = [None] * nx
    for k in range(kcount):
        scale = jnp.broadcast_to(coeffs[k], (ny, nz))
        for i in range(nx):
            term = vec_ref[k, i].astype(jnp.float32) * scale
            rows[i] = term if rows[i] is None else rows[i] + term
    return rows


class Plan:
    def __init__(self, mesh, kcount, row_count, block):
        self.gx, self.gy = mesh.shape["gx"], mesh.shape["gy"]
        self.devices = self.gx * self.gy
        self.kcount, self.row_count, self.block = kcount, row_count, block
        self.held = row_count // kcount
        self.members = block // kcount
        self.piece = kcount // self.gx
        self.lines = self.piece * block // LANES
        assert self.piece * self.gx == kcount and self.lines * LANES == self.piece * block
        assert self.gx % 2 == 0 and self.gy % 2 == 0


def invert(slots_ref, inv_ref):
    def body(t, carry):
        inv_ref[slots_ref[t]] = t
        return carry

    lax.fori_loop(0, slots_ref.shape[0], body, 0, unroll=slots_ref.shape[0] <= 64)


def coarse(plan, slots_ref, inv_ref, recv_p_ref, recv_w_ref, count):
    me = lax.axis_index("gx") * plan.gy + lax.axis_index("gy")
    slot = slots_ref[me]
    first = slot // plan.members * plan.members
    holder = slot * plan.kcount // plan.row_count
    group = lane_group(plan.kcount)
    groups = LANES // plan.kcount
    wide = max(1, plan.block // LANES)
    rhs = []
    for q in range(wide):
        row = None
        for g in range(groups):
            m = (q * LANES + g * plan.kcount) % plan.block // plan.kcount
            part = recv_p_ref[inv_ref[first + m], :, 0:LANES]
            row = part if row is None else jnp.where(group == g, part, row)
        rhs.append(row)
    coeffs = []
    split = max(1, LANES // plan.block)
    part_of = lane_group(LANES // split)
    for c in range(plan.gx):
        src = c * plan.gy + holder
        lines = [
            recv_w_ref[src, :, LANES * (1 + a):LANES * (2 + a)] * rhs[a % wide]
            for a in range(plan.lines)
        ]
        if wide > 1:
            lines = [sum(lines[a + 1:a + wide], lines[a]) for a in range(0, plan.lines, wide)]
        for line in lines:
            for s in range(split):
                piece = jnp.where(part_of == s, line, 0.0) if split > 1 else line
                coeffs.append(jnp.sum(piece, axis=1, keepdims=True))
    return [jnp.where(k < count, v, 0.0) for k, v in enumerate(coeffs)]


def pick(parity, low, high):
    even = parity == 0
    return jnp.where(even, high, low), jnp.where(even, low, high)


def prep_kernel(rhs_ref, diag_ref, solid_ref, centre_ref, fluid_ref, a_ref, b_ref):
    nx, ny, _ = rhs_ref.shape
    parity = lax.axis_index("gy") % 2
    fluid = 1.0 - solid_ref[...].astype(jnp.float32)
    centre = fluid * (6.0 + diag_ref[...]) + 1.0 - fluid
    fluid_ref[...] = fluid
    centre_ref[...] = centre
    for f, value in enumerate((centre, fluid, rhs_ref[...])):
        a, b = pick(parity, value[:, :H], value[:, ny - H:])
        a_ref[f * nx:(f + 1) * nx] = a
        b_ref[f * nx:(f + 1) * nx] = b


def first_kernel(plan, slots_ref, count_ref, rhs_ref, vec_ref, inv_rows_ref, msg_ref, inv_ref):
    nx = rhs_ref.shape[0]
    invert(slots_ref, inv_ref)
    proj = project(vec_ref, [rhs_ref[i] for i in range(nx)], count_ref[0, 0])
    msg_ref[:, :, 0:LANES] = jnp.broadcast_to(proj[None], (plan.devices, 1, LANES))
    gx, gy = lax.axis_index("gx"), lax.axis_index("gy")
    for k in range(plan.held):
        dest = inv_ref[gy * plan.held + k]
        rows = inv_rows_ref[k * plan.gx + gx]
        for a in range(plan.lines):
            msg_ref[dest, :, LANES * (1 + a):LANES * (2 + a)] = rows[a:a + 1]


def widen(own, a, b, parity):
    even = parity == 0
    return jnp.concatenate([jnp.where(even, b, a), own, jnp.where(even, a, b)], axis=1)


def static_mid_kernel(size, rhs_ref, centre_ref, fluid_ref, ya_ref, yb_ref,
                      c_ref, f_ref, r_ref, a_ref, b_ref):
    nx, ny, _ = rhs_ref.shape
    gy = lax.axis_index("gy")
    fields = []
    for f, own in enumerate((centre_ref, fluid_ref, rhs_ref)):
        part = slice(f * nx, (f + 1) * nx)
        fields.append(widen(own[...], ya_ref[part], yb_ref[part], gy % 2))
    centre, fluid, rhs = fields
    col = lax.broadcasted_iota(jnp.int32, centre.shape, 1)
    out = ((col < H) & (gy == 0)) | ((col >= ny + H) & (gy == size - 1))
    c_ref[...] = jnp.where(out, 1.0, centre)
    f_ref[...] = jnp.where(out, 0.0, fluid)
    r_ref[...] = rhs
    low = lax.axis_index("gx") % 2
    high = 1 - low
    at = 0
    for ref, width in ((c_ref, H), (f_ref, H), (r_ref, HR)):
        a_ref[at:at + width] = ref[pl.ds(high * (nx - width), width)]
        b_ref[at:at + width] = ref[pl.ds(low * (nx - width), width)]
        at += width


def start_kernel(size, c_ref, f_ref, r_ref, xa_ref, xb_ref,
                 centre_ref, fluid_ref, jacobi_ref, u_ref, rhs_ref):
    nx = c_ref.shape[0]
    ny = u_ref.shape[1]
    gx = lax.axis_index("gx")
    odd = gx % 2
    at = 0
    for own, ref, width in ((c_ref, centre_ref, H), (f_ref, fluid_ref, H), (r_ref, rhs_ref, HR)):
        ref[width:width + nx] = own[...]
        ref[pl.ds((1 - odd) * (nx + width), width)] = xa_ref[at:at + width]
        ref[pl.ds(odd * (nx + width), width)] = xb_ref[at:at + width]
        at += width

    @pl.when(gx == 0)
    def _():
        centre_ref[0:H] = jnp.ones_like(centre_ref[0:H])
        fluid_ref[0:H] = jnp.zeros_like(fluid_ref[0:H])

    @pl.when(gx == size - 1)
    def _():
        centre_ref[nx + H:] = jnp.ones_like(centre_ref[nx + H:])
        fluid_ref[nx + H:] = jnp.zeros_like(fluid_ref[nx + H:])

    jacobi_ref[...] = 1.0 / centre_ref[...]
    cut = H - HR
    span = range(cut, nx + 2 * H - cut)
    rows = smoother(
        [rhs_ref[i] for i in range(nx + 2 * HR)],
        [centre_ref[i] for i in span],
        [fluid_ref[i] for i in span],
        [jacobi_ref[i] for i in span],
    )
    for i in range(nx):
        u_ref[i] = rows[i][H:H + ny]


def direction_kernel(plan, slots_ref, count_ref, recv_ref, u_ref, rhs_ref, vec_ref,
                     d_ref, a_ref, b_ref, norm_ref, inv_ref):
    nx, ny, _ = u_ref.shape
    invert(slots_ref, inv_ref)
    coeffs = coarse(plan, slots_ref, inv_ref, recv_ref, recv_ref, count_ref[0, 0])
    rows = [u_ref[i] + f for i, f in enumerate(prolong(vec_ref, coeffs))]
    parity = lax.axis_index("gy") % 2
    for i in range(nx):
        d_ref[i] = rows[i]
        a_ref[i], b_ref[i] = pick(parity, rows[i][:H], rows[i][ny - H:])
    norm_ref[...] = jnp.broadcast_to(total([rhs_ref[i] * rows[i] for i in range(nx)]), (1, LANES))


def direction_mid_kernel(d_ref, ya_ref, yb_ref, dy_ref, a_ref, b_ref):
    nx = d_ref.shape[0]
    dy_ref[...] = widen(d_ref[...], ya_ref[...], yb_ref[...], lax.axis_index("gy") % 2)
    low = lax.axis_index("gx") % 2
    a_ref[...] = dy_ref[pl.ds((1 - low) * (nx - H), H)]
    b_ref[...] = dy_ref[pl.ds(low * (nx - H), H)]


def image_kernel(count_ref, dy_ref, xa_ref, xb_ref, d_ref, centre_ref, fluid_ref, jacobi_ref,
                 vec_ref, norm_ref, w_ref, u_ref, au_ref, msg_ref, wide_ref):
    nx, ny, _ = d_ref.shape
    odd = lax.axis_index("gx") % 2
    wide_ref[H:H + nx] = dy_ref[...]
    wide_ref[pl.ds((1 - odd) * (nx + H), H)] = xa_ref[...]
    wide_ref[pl.ds(odd * (nx + H), H)] = xb_ref[...]
    span = range(nx + 2 * H)
    centre = [centre_ref[i] for i in span]
    fluid = [fluid_ref[i] for i in span]
    jacobi = [jacobi_ref[i] for i in span]
    image = operate([wide_ref[i] for i in span], centre, fluid)
    smooth = smoother(image, inner(centre, 1), inner(fluid, 1), inner(jacobi, 1))
    image_u = operate(smooth, inner(centre, 3), inner(fluid, 3))
    w = [row[H:H + ny] for row in inner(image, H - 1)]
    for i in range(nx):
        w_ref[i] = w[i]
        u_ref[i] = smooth[i + 1][H:H + ny]
        au_ref[i] = image_u[i][H:H + ny]
    proj = project(vec_ref, w, count_ref[0, 0])
    curve = total([d_ref[i] * w[i] for i in range(nx)])
    sums = jnp.where(lane_group(32) == 0, norm_ref[...], curve)
    msg_ref[:, :, 0:LANES] = jnp.broadcast_to(proj[None], (msg_ref.shape[0], 1, LANES))
    msg_ref[:, :, LANES:] = jnp.broadcast_to(sums[None], (msg_ref.shape[0], 1, LANES))


def fine_kernel(plan, slots_ref, count_ref, recv_ref, recv_w_ref, vec_ref, fluid_ref,
                f_ref, ya_ref, yb_ref, xa_ref, xb_ref, inv_ref):
    nx, ny, _ = f_ref.shape
    invert(slots_ref, inv_ref)
    coeffs = coarse(plan, slots_ref, inv_ref, recv_ref, recv_w_ref, count_ref[0, 0])
    rows = prolong(vec_ref, coeffs)
    for i in range(nx):
        f_ref[i] = rows[i]
    masked = [r * fluid_ref[i] for i, r in enumerate(rows)]
    parity = lax.axis_index("gy") % 2
    for i in range(nx):
        ya_ref[i], yb_ref[i] = pick(parity, masked[i][:1], masked[i][ny - 1:])
    a, b = pick(lax.axis_index("gx") % 2, masked[0], masked[nx - 1])
    xa_ref[0] = a
    xb_ref[0] = b


def finish_kernel(plan, f_ref, ya_ref, yb_ref, xa_ref, xb_ref, u_ref, au_ref, w_ref, rhs_ref,
                  centre_ref, fluid_ref, z_ref, az_ref, msg_ref):
    nx, ny, nz = f_ref.shape
    gx, gy = lax.axis_index("gx"), lax.axis_index("gy")
    even_x, even_y = gx % 2 == 0, gy % 2 == 0
    lowest = jnp.where(even_x, xb_ref[0], xa_ref[0])
    highest = jnp.where(even_x, xa_ref[0], xb_ref[0])
    lowest = jnp.where(gx == 0, 0.0, lowest)
    highest = jnp.where(gx == plan.gx - 1, 0.0, highest)
    fine = [f_ref[i] for i in range(nx)]
    fluid = [fluid_ref[i] for i in range(nx)]
    masked = [lowest] + [a * b for a, b in zip(fine, fluid)] + [highest]
    lane = lax.broadcasted_iota(jnp.int32, (ny, nz), 1)
    row = lax.broadcasted_iota(jnp.int32, (ny, nz), 0)
    one, two, three = [], [], []
    for i in range(nx):
        mid = masked[i + 1]
        ya, yb = ya_ref[i], yb_ref[i]
        left = jnp.where(gy == 0, 0.0, jnp.where(even_y, yb, ya))
        right = jnp.where(gy == plan.gy - 1, 0.0, jnp.where(even_y, ya, yb))
        near = masked[i] + masked[i + 2]
        near = near + jnp.where(row == 0, left, pltpu.roll(mid, 1, 0))
        near = near + jnp.where(row == ny - 1, right, pltpu.roll(mid, ny - 1, 0))
        near = near + jnp.where(lane == 0, 0.0, pltpu.roll(mid, 1, 1))
        near = near + jnp.where(lane == nz - 1, 0.0, pltpu.roll(mid, nz - 1, 1))
        z = u_ref[i] + fine[i]
        az = au_ref[i] + (centre_ref[i] * fine[i] - fluid[i] * near)
        z_ref[i] = z
        az_ref[i] = az
        one.append(rhs_ref[i] * z)
        two.append(w_ref[i] * z)
        three.append(z * az)
    group = lane_group(32)
    sums = jnp.where(group == 0, total(one), jnp.where(group == 1, total(two), total(three)))
    msg_ref[...] = jnp.broadcast_to(sums[None], msg_ref.shape)


def last_kernel(recv2_ref, recv3_ref, rhs_ref, d_ref, w_ref, z_ref, az_ref, x_ref, r_ref):
    nx, ny, nz = d_ref.shape
    first = jnp.sum(recv2_ref[:, :, LANES:], axis=0)
    second = jnp.sum(recv3_ref[...], axis=0)
    norm, curve = first[:, 0:1], first[:, 32:33]
    rz, wz, zaz = second[:, 0:1], second[:, 32:33], second[:, 64:65]
    step = norm / curve
    norm_new = norm - step * (rz + curve) + step * step * wz
    ratio = norm_new / norm
    along = curve - step * wz
    bend = along - step * wz + step * step * zaz
    bend = bend + 2.0 * ratio * along + ratio * ratio * curve
    step_new = norm_new / bend
    shape = (ny, nz)
    on_d = jnp.broadcast_to(step + step_new * (1.0 + ratio), shape)
    on_z = jnp.broadcast_to(step_new * step, shape)
    for i in range(nx):
        x_ref[i] = on_d * d_ref[i] - on_z * z_ref[i]
        r_ref[i] = rhs_ref[i] - (on_d * w_ref[i] - on_z * az_ref[i])


def swap(a, b, axis):
    n = lax.axis_size(axis)
    even = [(i, i ^ 1) for i in range(n)]
    odd = [(i, (i + 1) % n if i % 2 else (i - 1) % n) for i in range(n)]
    return lax.ppermute(a, axis, even), lax.ppermute(b, axis, odd)


def exchange(msg):
    return lax.all_to_all(msg, ("gx", "gy"), 0, 0, tiled=True)


def on_device(mesh, rhs, diagonal, solid, vectors, counts, slots, inverse):
    nx, ny, nz = rhs.shape
    plan = Plan(mesh, vectors.shape[0], inverse.shape[0], inverse.shape[1])
    cells = (nx, ny, nz)
    side = (nx, ny + 2 * H, nz)
    wide = (nx + 2 * H, ny + 2 * H, nz)
    n = plan.devices
    inv_scratch = [pltpu.SMEM((n,), jnp.int32)]
    with_plan = lambda body: functools.partial(body, plan)

    inv_rows = inverse.reshape(plan.held * plan.gx, plan.lines, LANES)
    face = (3 * nx, H, nz)
    centre, fluid, a, b = call(prep_kernel, [cells, cells, face, face], rhs, diagonal, solid)
    ya, yb = swap(a, b, "gy")
    (msg1,) = call(with_plan(first_kernel), [(n, 1, LANES * (1 + plan.lines))],
                   slots, counts, rhs, vectors, inv_rows, scratch=inv_scratch, smem=2)
    recv1 = exchange(msg1)
    face = (2 * H + HR, ny + 2 * H, nz)
    c_y, f_y, r_y, a, b = call(functools.partial(static_mid_kernel, plan.gy),
                               [side, side, side, face, face], rhs, centre, fluid, ya, yb)
    xa, xb = swap(a, b, "gx")
    c_w, f_w, j_w, smooth, _ = call(functools.partial(start_kernel, plan.gx),
                                    [wide, wide, wide, cells, (nx + 2 * HR, ny + 2 * H, nz)],
                                    c_y, f_y, r_y, xa, xb)
    face = (nx, H, nz)
    direction, a, b, norm = call(with_plan(direction_kernel), [cells, face, face, (1, LANES)],
                                 slots, counts, recv1, smooth, rhs, vectors,
                                 scratch=inv_scratch, smem=2)
    ya, yb = swap(a, b, "gy")
    face = (H, ny + 2 * H, nz)
    d_y, a, b = call(direction_mid_kernel, [side, face, face], direction, ya, yb)
    xa, xb = swap(a, b, "gx")
    image, smooth, image_u, msg2 = call(
        image_kernel, [cells, cells, cells, (n, 1, 2 * LANES)],
        counts, d_y, xa, xb, direction, c_w, f_w, j_w, vectors, norm,
        scratch=[pltpu.VMEM(wide, jnp.float32)], smem=1)
    recv2 = exchange(msg2)
    fine, ya, yb, xa, xb = call(
        with_plan(fine_kernel), [cells, (nx, 1, nz), (nx, 1, nz), (1, ny, nz), (1, ny, nz)],
        slots, counts, recv2, recv1, vectors, fluid, scratch=inv_scratch, smem=2)
    ya, yb = swap(ya, yb, "gy")
    xa, xb = swap(xa, xb, "gx")
    z, image_z, msg3 = call(with_plan(finish_kernel), [cells, cells, (n, 1, LANES)],
                            fine, ya, yb, xa, xb, smooth, image_u, image, rhs, centre, fluid)
    recv3 = exchange(msg3)
    return tuple(call(last_kernel, [cells, cells],
                      recv2, recv3, rhs, direction, image, z, image_z))


def solution(mesh):
    in_specs = (
        P("gx", "gy", None),
        P("gx", "gy", None),
        P("gx", "gy", None),
        P(None, "gx", "gy", None),
        P("gx", "gy"),
        P(),
        P("gy", None),
    )
    out_specs = (P("gx", "gy", None), P("gx", "gy", None))
    return jax.shard_map(
        functools.partial(on_device, mesh), mesh=mesh, in_specs=in_specs, out_specs=out_specs,
        check_vma=False,
    )
```

time: 306 us -> 84.7 us (0.28)
  blocking collectives: 195 us -> 22.5 us
  starting transfers between devices: 57 us -> 20.6 us
  Pallas kernels: 0 us -> 20.7 us
  matrix products: 13 us -> 0 us
  other arithmetic: 9.63 us -> 0 us
  between operations: 10 us -> 1.37 us
  local copies, waits for them, and re-layouts: 8.08 us -> 4.49 us
    unnamed x2 -> x0, blocking collectives: 88.1 us -> none
    psum x2 -> x0, blocking collectives: 87.5 us -> none  [products(): lax.psum((jnp.sum(resid * pre), jnp.sum(pre * pre_image)), ('gx', 'gy'))]
    ppermute x24 -> x12, starting transfers between devices: 57 us -> 16.7 us  [swap(): return (lax.ppermute(a, axis, even), lax.ppermute(b, axis, odd))]
    all_to_all x0 -> x2, blocking collectives: none -> 22.5 us  [exchange(): return lax.all_to_all(msg, ('gx', 'gy'), 0, 0, tiled=True)]
    pallas_call x0 -> x10, Pallas kernels: none -> 20.7 us  [call(): pl.pallas_call(body, out_shape=shapes, in_specs=[SMEM] * smem + [VMEM] *...]
    all_gather x2 -> x0, blocking collectives: 19.1 us -> none  [precondition(): coarse_full = lax.all_gather(coarse_part, 'gy', axis=0, tiled=True)]
    dot_general x4 -> x0, matrix products: 13 us -> none  [the longest x2 7.52 us: precondition(): fine = jnp.dot(coeffs, vec_matrix, precision=HIGH)]
    unnamed x2 -> x0, other arithmetic: 4 us -> none
  transfers between devices with their start and end apart: 24 -> 13, of which waited for: 5 -> 8; matrix products, arithmetic and copies ran while one was open for 9% -> 1% of each run, Pallas kernels for 0% -> 7%
where the time goes in v1:
time: 84.7 us; the launch traced here: 84.1 us
  blocking collectives  22.5 us (27%)
  Pallas kernels  20.7 us (24%)
  starting transfers between devices  20.6 us (24%)
  waiting for transfers between devices  14.5 us (17%)
  local copies, waits for them, and re-layouts  4.49 us (5%)
  between operations  1.37 us (2%)
    all_to_all x2, blocking collectives, exchange(): return lax.all_to_all(msg, ('gx', 'gy'), 0, 0, tiled=True)  22.5 us
    pallas_call x10, Pallas kernels, call(): pl.pallas_call(body, out_shape=shapes, in_specs=[SMEM] * smem + [VMEM] *...  20.7 us
    ppermute x12, starting transfers between devices, swap(): return (lax.ppermute(a, axis, even), lax.ppermute(b, axis, odd))  16.7 us
    ppermute x12, waiting for transfers between devices, swap(): return (lax.ppermute(a, axis, even), lax.ppermute(b, axis, odd))  14.5 us
    all_to_all x1, starting transfers between devices, exchange(): return lax.all_to_all(msg, ('gx', 'gy'), 0, 0, tiled=True)  3.97 us
    unnamed x31, local copies, waits for them, and re-layouts  3.79 us
  transfers between devices with their start and end apart: 13, of which 8 were waited for; matrix products, arithmetic and copies ran while one was open for 1% of the time, Pallas kernels for 7%

profile of v1, /device:TPU:0, one launch (start us, length us, event | category | flops | bytes accessed | tf_op | source)
XLA Modules:
  0.0 84.1 jit_solution(6827376355115008267)
XLA Ops:
  0.6 1.6 %shard_map.87 = (f32[8,16,128]{2,1,0:T(8,128)}, f32[8,16,128]{2,1,0:T(8,128)}, f32[24,4,128]{2,1,0:T(4,128)}, f32[24,4,128]{2,1,0:T(4,128)}) custom-call(f32[8,16,128]{2,1,0:T(8,128)} %rhs_ref.11, f32[8,16,128]{2,1,0:T(8,128)} %diag_ref.1, s32[8,16,128]{2,1,0:T(8,128)} %solid_ref.1), custom_call_target="tpu_custom_call" | custom-call | tf_op jit(solution)/shard_map/pallas_call | solution.py:22
  2.7 3.5 %collective-permute-start.1 = (f32[24,4,128]{2,1,0:T(4,128)}, f32[24,4,128]{2,1,0:T(4,128)S(1)}, u32[]{:S(2)}, u32[]{:S(2)}) collective-permute-start(f32[24,4,128]{2,1,0:T(4,128)} %get-tuple-element.37), channel_id=1, source_target_pairs={{0,7},{1,2},{2,1},{3,4},{4,3},{5,6},{6,5},{7,0},{8,15},{9,10},{10,... | collective-permute-start | bytes 147464 | tf_op jit(solution)/shard_map/ppermute | solution.py:392
  7.7 2.2 %shard_map.86 = f32[32,1,640]{2,1,0:T(1,128)} custom-call(s32[32]{0:T(128)} %slots_ref.5, s32[1,1]{1,0:T(1,128)S(6)} %copy.11.count_ref, f32[8,16,128]{2,1,0:T(8,128)} %rhs_ref.11, bf16[32,8,16,128]{3,2,1,0:T(8,128)(2,1)} %vec_ref.7, f32[16,4,128]{2,1,0:T(4,128)} %reshape.7.inv_rows_ref), custom_call_target="tpu_custom_call" | custom-call | tf_op jit(solution)/shard_map/pallas_call | solution.py:22
  9.9 4.0 %all-to-all-start = ((f32[32,1,640]{2,1,0:T(1,128)}), f32[32,1,640]{2,1,0:T(1,128)S(1)}, u32[]{:S(2)}, u32[]{:S(2)}) async-start(f32[32,1,640]{2,1,0:T(1,128)} %shard_map.86), calls=%async_computation | async-start | bytes 163840 | tf_op jit(solution)/shard_map/all_to_all | solution.py:396
  14.5 1.8 %shard_map.88 = (f32[8,24,128]{2,1,0:T(8,128)}, f32[8,24,128]{2,1,0:T(8,128)}, f32[8,24,128]{2,1,0:T(8,128)}, f32[10,24,128]{2,1,0:T(8,128)}, f32[10,24,128]{2,1,0:T(8,128)}) custom-call(f32[8,16,128]{2,1,0:T(8,128)} %rhs_ref.11, f32[8,16,128]{2,1,0:T(8,128)} %get-tuple-element.34.centre_ref, f32[8,16,128]{2,1,0:T(8,128)} %get-tuple-element.35.fluid_ref, ...), custom_call_target="tpu_custom_call" | custom-call | tf_op jit(solution)/shard_map/pallas_call | solution.py:22
  16.3 1.8 %collective-permute-start.2 = (f32[10,24,128]{2,1,0:T(8,128)}, f32[10,24,128]{2,1,0:T(8,128)S(1)}, u32[]{:S(2)}, u32[]{:S(2)}) collective-permute-start(f32[10,24,128]{2,1,0:T(8,128)} %get-tuple-element.41), channel_id=1, source_target_pairs={{0,8},{8,0},{16,24},{24,16},{1,9},{9,1},{17,25},{25,17},{2,10},{10... | collective-permute-start | bytes 368648 | tf_op jit(solution)/shard_map/ppermute | solution.py:392
  18.1 2.4 %collective-permute-start.3 = (f32[10,24,128]{2,1,0:T(8,128)}, f32[10,24,128]{2,1,0:T(8,128)S(1)}, u32[]{:S(2)}, u32[]{:S(2)}) collective-permute-start(f32[10,24,128]{2,1,0:T(8,128)} %get-tuple-element.42), channel_id=1, source_target_pairs={{0,24},{8,16},{16,8},{24,0},{1,25},{9,17},{17,9},{25,1},{2,26},{10... | collective-permute-start | bytes 368648 | tf_op jit(solution)/shard_map/ppermute | solution.py:392
  20.4 1.7 %collective-permute-done.2.xa_ref = f32[10,24,128]{2,1,0:T(8,128)S(1)} collective-permute-done((f32[10,24,128]{2,1,0:T(8,128)}, f32[10,24,128]{2,1,0:T(8,128)S(1)}, u32[]{:S(2)}, u32[]{:S(2)}) %collective-permute-start.2) | collective-permute-done | bytes 122912 | tf_op jit(solution)/shard_map/ppermute | solution.py:392
  22.2 4.5 %collective-permute-done.3.xb_ref = f32[10,24,128]{2,1,0:T(8,128)S(1)} collective-permute-done((f32[10,24,128]{2,1,0:T(8,128)}, f32[10,24,128]{2,1,0:T(8,128)S(1)}, u32[]{:S(2)}, u32[]{:S(2)}) %collective-permute-start.3) | collective-permute-done | bytes 122912 | tf_op jit(solution)/shard_map/ppermute | solution.py:392
  27.3 2.1 %shard_map.89 = (f32[16,24,128]{2,1,0:T(8,128)}, f32[16,24,128]{2,1,0:T(8,128)}, f32[16,24,128]{2,1,0:T(8,128)}, f32[8,16,128]{2,1,0:T(8,128)}, f32[12,24,128]{2,1,0:T(8,128)}) custom-call(f32[8,24,128]{2,1,0:T(8,128)} %get-tuple-element.38.c_ref, f32[8,24,128]{2,1,0:T(8,128)} %get-tuple-element.39.f_ref, f32[8,24,128]{2,1,0:T(8,128)} %get-tuple-element.40.r_ref, ...), custom_call_target="tpu_custom_call" | custom-call | tf_op jit(solution)/shard_map/pallas_call | solution.py:22
  30.0 2.4 %shard_map.90 = (f32[8,16,128]{2,1,0:T(8,128)}, f32[8,4,128]{2,1,0:T(4,128)}, f32[8,4,128]{2,1,0:T(4,128)}, f32[1,128]{1,0:T(1,128)}) custom-call(s32[32]{0:T(128)} %slots_ref.5, s32[1,1]{1,0:T(1,128)S(6)} %copy.11.count_ref, f32[32,1,640]{2,1,0:T(1,128)} %copy-done, f32[8,16,128]{2,1,0:T(8,128)} %get-tuple-element.43.u_ref, f32[8,16,128]{2,1,0:T(8,128)} %rhs_ref.11, ...), custom_call_target="tpu_custom_call" | custom-call | tf_op jit(solution)/shard_map/pallas_call | solution.py:22
  32.4 2.5 %collective-permute-start.5 = (f32[8,4,128]{2,1,0:T(4,128)}, f32[8,4,128]{2,1,0:T(4,128)S(1)}, u32[]{:S(2)}, u32[]{:S(2)}) collective-permute-start(f32[8,4,128]{2,1,0:T(4,128)} %get-tuple-element.46), channel_id=1, source_target_pairs={{0,7},{1,2},{2,1},{3,4},{4,3},{5,6},{6,5},{7,0},{8,15},{9,10},{10,... | collective-permute-start | bytes 49160 | tf_op jit(solution)/shard_map/ppermute | solution.py:392
  34.9 1.8 %collective-permute-done.5.yb_ref = f32[8,4,128]{2,1,0:T(4,128)S(1)} collective-permute-done((f32[8,4,128]{2,1,0:T(4,128)}, f32[8,4,128]{2,1,0:T(4,128)S(1)}, u32[]{:S(2)}, u32[]{:S(2)}) %collective-permute-start.5) | collective-permute-done | bytes 16416 | tf_op jit(solution)/shard_map/ppermute | solution.py:392
  37.3 1.6 %shard_map.91 = (f32[8,24,128]{2,1,0:T(8,128)}, f32[4,24,128]{2,1,0:T(8,128)}, f32[4,24,128]{2,1,0:T(8,128)}) custom-call(f32[8,16,128]{2,1,0:T(8,128)} %get-tuple-element.44.d_ref, f32[8,4,128]{2,1,0:T(4,128)} %copy-done.8, f32[8,4,128]{2,1,0:T(4,128)} %copy-done.9), custom_call_target="tpu_custom_call" | custom-call | tf_op jit(solution)/shard_map/pallas_call | solution.py:22
  38.9 3.2 %collective-permute-start.7 = (f32[4,24,128]{2,1,0:T(8,128)}, f32[4,24,128]{2,1,0:T(8,128)S(1)}, u32[]{:S(2)}, u32[]{:S(2)}) collective-permute-start(f32[4,24,128]{2,1,0:T(8,128)} %get-tuple-element.49), channel_id=1, source_target_pairs={{0,24},{8,16},{16,8},{24,0},{1,25},{9,17},{17,9},{25,1},{2,26},{10... | collective-permute-start | bytes 147464 | tf_op jit(solution)/shard_map/ppermute | solution.py:392
  43.2 1.9 %collective-permute-done.7.xb_ref = f32[4,24,128]{2,1,0:T(8,128)S(1)} collective-permute-done((f32[4,24,128]{2,1,0:T(8,128)}, f32[4,24,128]{2,1,0:T(8,128)S(1)}, u32[]{:S(2)}, u32[]{:S(2)}) %collective-permute-start.7) | collective-permute-done | bytes 49184 | tf_op jit(solution)/shard_map/ppermute | solution.py:392
  45.7 2.8 %shard_map.92 = (f32[8,16,128]{2,1,0:T(8,128)}, f32[8,16,128]{2,1,0:T(8,128)}, f32[8,16,128]{2,1,0:T(8,128)}, f32[32,1,256]{2,1,0:T(1,128)}) custom-call(s32[1,1]{1,0:T(1,128)S(6)} %copy.11.count_ref, f32[8,24,128]{2,1,0:T(8,128)} %get-tuple-element.47.dy_ref, f32[4,24,128]{2,1,0:T(8,128)} %copy-done.5, f32[4,24,128]{2,1,0:T(8,128)} %copy-done.6, ...), custom_call_target="tpu_custom_call" | custom-call | tf_op jit(solution)/shard_map/pallas_call | solution.py:22
  48.5 12.2 %all_to_all.15.recv_ref.recv2_ref = f32[32,1,256]{2,1,0:T(1,128)} all-to-all(f32[32,1,256]{2,1,0:T(1,128)} %get-tuple-element.54), channel_id=1, replica_groups=mesh['gx'=4,'gy'=8] {'gx','gy'}, dimensions={0} | all-to-all | bytes 65536 | tf_op jit(solution)/shard_map/all_to_all | solution.py:396
  60.7 2.3 %shard_map.93 = (f32[8,16,128]{2,1,0:T(8,128)}, f32[8,1,128]{2,1,0:T(1,128)}, f32[8,1,128]{2,1,0:T(1,128)}, f32[1,16,128]{2,1,0:T(8,128)}, f32[1,16,128]{2,1,0:T(8,128)}) custom-call(s32[32]{0:T(128)} %slots_ref.5, s32[1,1]{1,0:T(1,128)S(6)} %copy.11.count_ref, f32[32,1,256]{2,1,0:T(1,128)} %all_to_all.15.recv_ref.recv2_ref, f32[32,1,640]{2,1,0:T(1,128)} %copy-done, ...), custom_call_target="tpu_custom_call" | custom-call | tf_op jit(solution)/shard_map/pallas_call | solution.py:22
  63.6 1.5 %collective-permute-start.11 = (f32[1,16,128]{2,1,0:T(8,128)}, f32[1,16,128]{2,1,0:T(8,128)S(1)}, u32[]{:S(2)}, u32[]{:S(2)}) collective-permute-start(f32[1,16,128]{2,1,0:T(8,128)} %get-tuple-element.59), channel_id=1, source_target_pairs={{0,24},{8,16},{16,8},{24,0},{1,25},{9,17},{17,9},{25,1},{2,26},{10... | collective-permute-start | bytes 24584 | tf_op jit(solution)/shard_map/ppermute | solution.py:392
  66.5 2.6 %collective-permute-done.9.yb_ref = f32[8,1,128]{2,1,0:T(1,128)S(1)} collective-permute-done((f32[8,1,128]{2,1,0:T(1,128)S(1)}, f32[8,1,128]{2,1,0:T(1,128)S(1)}, u32[]{:S(2)}, u32[]{:S(2)}) %collective-permute-start.9) | collective-permute-done | bytes 4128 | tf_op jit(solution)/shard_map/ppermute | solution.py:392
  69.9 1.9 %shard_map.94 = (f32[8,16,128]{2,1,0:T(8,128)}, f32[8,16,128]{2,1,0:T(8,128)}, f32[32,1,128]{2,1,0:T(1,128)}) custom-call(f32[8,16,128]{2,1,0:T(8,128)} %get-tuple-element.55.f_ref, f32[8,1,128]{2,1,0:T(1,128)} %copy-done.12, f32[8,1,128]{2,1,0:T(1,128)} %copy-done.13, f32[1,16,128]{2,1,0:T(8,128)} %copy-done.10, f32[1,16,128]{2,1,0:T(8,128)} %copy-done.11, ...), custom_call_target="tpu_custom_call" | custom-call | tf_op jit(solution)/shard_map/pallas_call | solution.py:22
  71.8 10.3 %all_to_all.16.recv3_ref = f32[32,1,128]{2,1,0:T(1,128)} all-to-all(f32[32,1,128]{2,1,0:T(1,128)} %get-tuple-element.63), channel_id=1, replica_groups=mesh['gx'=4,'gy'=8] {'gx','gy'}, dimensions={0} | all-to-all | bytes 32768 | tf_op jit(solution)/shard_map/all_to_all | solution.py:396
  82.0 2.1 %shard_map.95 = (f32[8,16,128]{2,1,0:T(8,128)}, f32[8,16,128]{2,1,0:T(8,128)}) custom-call(f32[32,1,256]{2,1,0:T(1,128)} %all_to_all.15.recv_ref.recv2_ref, f32[32,1,128]{2,1,0:T(1,128)} %all_to_all.16.recv3_ref, f32[8,16,128]{2,1,0:T(8,128)} %rhs_ref.11, f32[8,16,128]{2,1,0:T(8,128)} %get-tuple-element.44.d_ref, f32[8,16,128]{2,1,0:T(8,128)} %get-tuple-element.62.w_ref, ...), custom_call_target="tpu_custom_call" | custom-call | tf_op jit(solution)/shard_map/pallas_call | solution.py:22
  (46 shorter events, 8.3 us)
Async XLA Ops:
  0.6 6.3 %copy-start.7 = (f32[128,64]{0,1:T(8,128)S(1)}, f32[128,64]{0,1:T(8,128)}, u32[]{:S(2)}) copy-start(f32[128,64]{0,1:T(8,128)} %param.13) | copy-start | bytes 98308
  2.2 11.7 %collective-permute-start = (f32[24,4,128]{2,1,0:T(4,128)}, f32[24,4,128]{2,1,0:T(4,128)S(1)}, u32[]{:S(2)}, u32[]{:S(2)}) collective-permute-start(f32[24,4,128]{2,1,0:T(4,128)} %get-tuple-element.36), channel_id=1, source_target_pairs={{0,1},{1,0},{2,3},{3,2},{4,5},{5,4},{6,7},{7,6},{8,9},{9,8},{10,11... | collective-permute-start | bytes 147464 | tf_op jit(solution)/shard_map/ppermute | solution.py:392
  2.7 11.2 %collective-permute-start.1 = (f32[24,4,128]{2,1,0:T(4,128)}, f32[24,4,128]{2,1,0:T(4,128)S(1)}, u32[]{:S(2)}, u32[]{:S(2)}) collective-permute-start(f32[24,4,128]{2,1,0:T(4,128)} %get-tuple-element.37), channel_id=1, source_target_pairs={{0,7},{1,2},{2,1},{3,4},{4,3},{5,6},{6,5},{7,0},{8,15},{9,10},{10,... | collective-permute-start | bytes 147464 | tf_op jit(solution)/shard_map/ppermute | solution.py:392
  9.9 19.5 %all-to-all-start = ((f32[32,1,640]{2,1,0:T(1,128)}), f32[32,1,640]{2,1,0:T(1,128)S(1)}, u32[]{:S(2)}, u32[]{:S(2)}) async-start(f32[32,1,640]{2,1,0:T(1,128)} %shard_map.86), calls=%async_computation | async-start | bytes 163840 | tf_op jit(solution)/shard_map/all_to_all | solution.py:396
  13.9 0.6 copy-start.3
  13.9 0.6 copy-start.4
  16.3 5.9 %collective-permute-start.2 = (f32[10,24,128]{2,1,0:T(8,128)}, f32[10,24,128]{2,1,0:T(8,128)S(1)}, u32[]{:S(2)}, u32[]{:S(2)}) collective-permute-start(f32[10,24,128]{2,1,0:T(8,128)} %get-tuple-element.41), channel_id=1, source_target_pairs={{0,8},{8,0},{16,24},{24,16},{1,9},{9,1},{17,25},{25,17},{2,10},{10... | collective-permute-start | bytes 368648 | tf_op jit(solution)/shard_map/ppermute | solution.py:392
  18.1 8.6 %collective-permute-start.3 = (f32[10,24,128]{2,1,0:T(8,128)}, f32[10,24,128]{2,1,0:T(8,128)S(1)}, u32[]{:S(2)}, u32[]{:S(2)}) collective-permute-start(f32[10,24,128]{2,1,0:T(8,128)} %get-tuple-element.42), channel_id=1, source_target_pairs={{0,24},{8,16},{16,8},{24,0},{1,25},{9,17},{17,9},{25,1},{2,26},{10... | collective-permute-start | bytes 368648 | tf_op jit(solution)/shard_map/ppermute | solution.py:392
  22.2 4.5 %copy-start.1 = (f32[10,24,128]{2,1,0:T(8,128)}, f32[10,24,128]{2,1,0:T(8,128)S(1)}, u32[]{:S(2)}) copy-start(f32[10,24,128]{2,1,0:T(8,128)S(1)} %collective-permute-done.2.xa_ref) | copy-start | bytes 368644
  26.7 0.6 copy-start.2
  29.4 0.6 copy-start
  32.4 2.5 %collective-permute-start.4 = (f32[8,4,128]{2,1,0:T(4,128)}, f32[8,4,128]{2,1,0:T(4,128)S(1)}, u32[]{:S(2)}, u32[]{:S(2)}) collective-permute-start(f32[8,4,128]{2,1,0:T(4,128)} %get-tuple-element.45), channel_id=1, source_target_pairs={{0,1},{1,0},{2,3},{3,2},{4,5},{5,4},{6,7},{7,6},{8,9},{9,8},{10,11... | collective-permute-start | bytes 49160 | tf_op jit(solution)/shard_map/ppermute | solution.py:392
  32.4 4.3 %collective-permute-start.5 = (f32[8,4,128]{2,1,0:T(4,128)}, f32[8,4,128]{2,1,0:T(4,128)S(1)}, u32[]{:S(2)}, u32[]{:S(2)}) collective-permute-start(f32[8,4,128]{2,1,0:T(4,128)} %get-tuple-element.46), channel_id=1, source_target_pairs={{0,7},{1,2},{2,1},{3,4},{4,3},{5,6},{6,5},{7,0},{8,15},{9,10},{10,... | collective-permute-start | bytes 49160 | tf_op jit(solution)/shard_map/ppermute | solution.py:392
  34.9 1.8 %copy-start.8 = (f32[8,4,128]{2,1,0:T(4,128)}, f32[8,4,128]{2,1,0:T(4,128)S(1)}, u32[]{:S(2)}) copy-start(f32[8,4,128]{2,1,0:T(4,128)S(1)} %collective-permute-done.4.ya_ref) | copy-start | bytes 49156
  38.9 4.3 %collective-permute-start.6 = (f32[4,24,128]{2,1,0:T(8,128)}, f32[4,24,128]{2,1,0:T(8,128)S(1)}, u32[]{:S(2)}, u32[]{:S(2)}) collective-permute-start(f32[4,24,128]{2,1,0:T(8,128)} %get-tuple-element.48), channel_id=1, source_target_pairs={{0,8},{8,0},{16,24},{24,16},{1,9},{9,1},{17,25},{25,17},{2,10},{10... | collective-permute-start | bytes 147464 | tf_op jit(solution)/shard_map/ppermute | solution.py:392
  38.9 6.2 %collective-permute-start.7 = (f32[4,24,128]{2,1,0:T(8,128)}, f32[4,24,128]{2,1,0:T(8,128)S(1)}, u32[]{:S(2)}, u32[]{:S(2)}) collective-permute-start(f32[4,24,128]{2,1,0:T(8,128)} %get-tuple-element.49), channel_id=1, source_target_pairs={{0,24},{8,16},{16,8},{24,0},{1,25},{9,17},{17,9},{25,1},{2,26},{10... | collective-permute-start | bytes 147464 | tf_op jit(solution)/shard_map/ppermute | solution.py:392
  43.2 1.9 %copy-start.5 = (f32[4,24,128]{2,1,0:T(8,128)}, f32[4,24,128]{2,1,0:T(8,128)S(1)}, u32[]{:S(2)}) copy-start(f32[4,24,128]{2,1,0:T(8,128)S(1)} %collective-permute-done.6.xa_ref) | copy-start | bytes 147460
  45.1 0.6 copy-start.6
  63.0 2.1 %copy-start.14 = (f32[8,1,128]{2,1,0:T(1,128)S(1)}, f32[8,1,128]{2,1,0:T(1,128)}, u32[]{:S(2)}) copy-start(f32[8,1,128]{2,1,0:T(1,128)} %get-tuple-element.57) | copy-start | bytes 12292
  63.0 6.0 %collective-permute-start.10 = (f32[1,16,128]{2,1,0:T(8,128)}, f32[1,16,128]{2,1,0:T(8,128)S(1)}, u32[]{:S(2)}, u32[]{:S(2)}) collective-permute-start(f32[1,16,128]{2,1,0:T(8,128)} %get-tuple-element.58), channel_id=1, source_target_pairs={{0,8},{8,0},{16,24},{24,16},{1,9},{9,1},{17,25},{25,17},{2,10},{10... | collective-permute-start | bytes 24584 | tf_op jit(solution)/shard_map/ppermute | solution.py:392
  63.6 5.7 %collective-permute-start.11 = (f32[1,16,128]{2,1,0:T(8,128)}, f32[1,16,128]{2,1,0:T(8,128)S(1)}, u32[]{:S(2)}, u32[]{:S(2)}) collective-permute-start(f32[1,16,128]{2,1,0:T(8,128)} %get-tuple-element.59), channel_id=1, source_target_pairs={{0,24},{8,16},{16,8},{24,0},{1,25},{9,17},{17,9},{25,1},{2,26},{10... | collective-permute-start | bytes 24584 | tf_op jit(solution)/shard_map/ppermute | solution.py:392
  65.1 1.4 %collective-permute-start.8 = (f32[8,1,128]{2,1,0:T(1,128)}, f32[8,1,128]{2,1,0:T(1,128)S(1)}, u32[]{:S(2)}, u32[]{:S(2)}) collective-permute-start(f32[8,1,128]{2,1,0:T(1,128)} %get-tuple-element.56), channel_id=1, source_target_pairs={{0,1},{1,0},{2,3},{3,2},{4,5},{5,4},{6,7},{7,6},{8,9},{9,8},{10,11... | collective-permute-start | bytes 12296 | tf_op jit(solution)/shard_map/ppermute | solution.py:392
  65.1 3.9 %collective-permute-start.9 = (f32[8,1,128]{2,1,0:T(1,128)S(1)}, f32[8,1,128]{2,1,0:T(1,128)S(1)}, u32[]{:S(2)}, u32[]{:S(2)}) collective-permute-start(f32[8,1,128]{2,1,0:T(1,128)S(1)} %copy-done.14), channel_id=1, source_target_pairs={{0,7},{1,2},{2,1},{3,4},{4,3},{5,6},{6,5},{7,0},{8,15},{9,10},{10,... | collective-permute-start | bytes 12296 | tf_op jit(solution)/shard_map/ppermute | solution.py:392
  66.5 2.8 %copy-start.12 = (f32[8,1,128]{2,1,0:T(1,128)}, f32[8,1,128]{2,1,0:T(1,128)S(1)}, u32[]{:S(2)}) copy-start(f32[8,1,128]{2,1,0:T(1,128)S(1)} %collective-permute-done.8.ya_ref) | copy-start | bytes 12292
  (4 other events, 2.4 us)

commit v2 on v1

--- a/solution.py
+++ b/solution.py
@@ -13,6 +13,7 @@
 H = 4
 HR = 2
 LANES = 128
+VMEM_GRANT = 16 * 2**20
 VMEM = pl.BlockSpec(memory_space=pltpu.VMEM)
 SMEM = pl.BlockSpec(memory_space=pltpu.SMEM)
 
@@ -25,6 +26,7 @@
         in_specs=[SMEM] * smem + [VMEM] * (len(args) - smem),
         out_specs=[VMEM] * len(out),
         scratch_shapes=list(scratch),
+        compiler_params=pltpu.CompilerParams(vmem_limit_bytes=VMEM_GRANT),
     )(*args)
 
 

time: 84.7 us -> 69.1 us (0.82)
  Pallas kernels: 20.7 us -> 6.25 us
  blocking collectives: 22.5 us -> 20.7 us
  waiting for transfers between devices: 14.5 us -> 15.7 us
    pallas_call x10, Pallas kernels: 20.7 us -> 6.25 us  [call(): pl.pallas_call(body, out_shape=shapes, in_specs=[SMEM] * smem + [VMEM] *...]
    all_to_all x2, blocking collectives: 22.5 us -> 20.7 us  [exchange(): return lax.all_to_all(msg, ('gx', 'gy'), 0, 0, tiled=True)]
    ppermute x12, waiting for transfers between devices: 14.5 us -> 15.7 us  [swap(): return (lax.ppermute(a, axis, even), lax.ppermute(b, axis, odd))]
    unnamed x31 -> x17, local copies, waits for them, and re-layouts: 3.79 us -> 4.58 us
  transfers between devices with their start and end apart: 13 -> 13, of which waited for: 8 -> 7; matrix products, arithmetic and copies ran while one was open for 1% -> 0% of each run, Pallas kernels for 7% -> 3%
where the time goes in v2:
time: 69.1 us; the launch traced here: 68.7 us
  blocking collectives  20.7 us (30%)
  starting transfers between devices  19.9 us (29%)
  waiting for transfers between devices  15.7 us (23%)
  Pallas kernels  6.25 us (9%)
  local copies, waits for them, and re-layouts  4.67 us (7%)
  between operations  1.41 us (2%)
    all_to_all x2, blocking collectives, exchange(): return lax.all_to_all(msg, ('gx', 'gy'), 0, 0, tiled=True)  20.7 us
    ppermute x12, starting transfers between devices, swap(): return (lax.ppermute(a, axis, even), lax.ppermute(b, axis, odd))  16 us
    ppermute x12, waiting for transfers between devices, swap(): return (lax.ppermute(a, axis, even), lax.ppermute(b, axis, odd))  15.7 us
    pallas_call x10, Pallas kernels, call(): pl.pallas_call(body, out_shape=shapes, in_specs=[SMEM] * smem + [VMEM] *...  6.25 us
    unnamed x17, local copies, waits for them, and re-layouts  4.58 us
    all_to_all x1, starting transfers between devices, exchange(): return lax.all_to_all(msg, ('gx', 'gy'), 0, 0, tiled=True)  3.97 us
  transfers between devices with their start and end apart: 13, of which 7 were waited for; matrix products, arithmetic and copies ran while one was open for 0% of the time, Pallas kernels for 3%

profile of v2, /device:TPU:0, one launch (start us, length us, event | category | flops | bytes accessed | tf_op | source)
XLA Modules:
  0.0 68.7 jit_solution(10664189611071473760)
XLA Ops:
  0.6 0.8 %copy-done.2 = f32[8,16,128]{2,1,0:T(8,128)S(1)} copy-done((f32[8,16,128]{2,1,0:T(8,128)S(1)}, f32[8,16,128]{2,1,0:T(8,128)}, u32[]{:S(2)}) %copy-start.2) | copy-done | bytes 65560
  1.5 0.8 %copy-done.4 = f32[8,16,128]{2,1,0:T(8,128)S(1)} copy-done((f32[8,16,128]{2,1,0:T(8,128)S(1)}, f32[8,16,128]{2,1,0:T(8,128)}, u32[]{:S(2)}) %copy-start.4) | copy-done | bytes 65560
  2.3 0.8 %copy-done.5 = s32[8,16,128]{2,1,0:T(8,128)S(1)} copy-done((s32[8,16,128]{2,1,0:T(8,128)S(1)}, s32[8,16,128]{2,1,0:T(8,128)}, u32[]{:S(2)}) %copy-start.5) | copy-done | bytes 65560
  3.7 3.5 %collective-permute-start.1 = (f32[24,4,128]{2,1,0:T(4,128)S(1)}, f32[24,4,128]{2,1,0:T(4,128)S(1)}, u32[]{:S(2)}, u32[]{:S(2)}) collective-permute-start(f32[24,4,128]{2,1,0:T(4,128)S(1)} %get-tuple-element.37), channel_id=1, source_target_pairs={{0,7},{1,2},{2,1},{3,4},{4,3},{5,6},{6,5},{7,0},{8,15},{9,10},{10,... | collective-permute-start | bytes 147464 | tf_op jit(solution)/shard_map/ppermute | solution.py:394
  8.9 1.2 %copy-done = bf16[32,8,16,128]{3,2,1,0:T(8,128)(2,1)S(1)} copy-done((bf16[32,8,16,128]{3,2,1,0:T(8,128)(2,1)S(1)}, bf16[32,8,16,128]{3,2,1,0:T(8,128)(2,1)}, u32[]{:S(2)}) %copy-start) | copy-done | bytes 1048600
  10.1 1.5 %shard_map.86 = f32[32,1,640]{2,1,0:T(1,128)} custom-call(s32[32]{0:T(128)S(1)} %copy-done.6, s32[1,1]{1,0:T(1,128)S(6)} %copy.11.count_ref, f32[8,16,128]{2,1,0:T(8,128)S(1)} %copy-done.3, bf16[32,8,16,128]{3,2,1,0:T(8,128)(2,1)S(1)} %copy-done, f32[16,4,128]{2,1,0:T(4,128)S(1)} %reshape.7.inv_rows_ref), custom_call_target="tpu_custom_call" | custom-call | tf_op jit(solution)/shard_map/pallas_call | solution.py:23
  11.6 4.0 %all-to-all-start = ((f32[32,1,640]{2,1,0:T(1,128)}), f32[32,1,640]{2,1,0:T(1,128)S(1)}, u32[]{:S(2)}, u32[]{:S(2)}) async-start(f32[32,1,640]{2,1,0:T(1,128)} %shard_map.86), calls=%async_computation | async-start | bytes 163840 | tf_op jit(solution)/shard_map/all_to_all | solution.py:398
  15.7 1.8 %collective-permute-start.2 = (f32[10,24,128]{2,1,0:T(8,128)S(1)}, f32[10,24,128]{2,1,0:T(8,128)S(1)}, u32[]{:S(2)}, u32[]{:S(2)}) collective-permute-start(f32[10,24,128]{2,1,0:T(8,128)S(1)} %get-tuple-element.41), channel_id=1, source_target_pairs={{0,8},{8,0},{16,24},{24,16},{1,9},{9,1},{17,25},{25,17},{2,10},{10... | collective-permute-start | bytes 368648 | tf_op jit(solution)/shard_map/ppermute | solution.py:394
  17.5 2.4 %collective-permute-start.3 = (f32[10,24,128]{2,1,0:T(8,128)S(1)}, f32[10,24,128]{2,1,0:T(8,128)S(1)}, u32[]{:S(2)}, u32[]{:S(2)}) collective-permute-start(f32[10,24,128]{2,1,0:T(8,128)S(1)} %get-tuple-element.42), channel_id=1, source_target_pairs={{0,24},{8,16},{16,8},{24,0},{1,25},{9,17},{17,9},{25,1},{2,26},{10... | collective-permute-start | bytes 368648 | tf_op jit(solution)/shard_map/ppermute | solution.py:394
  19.9 2.5 %collective-permute-done.2.xa_ref = f32[10,24,128]{2,1,0:T(8,128)S(1)} collective-permute-done((f32[10,24,128]{2,1,0:T(8,128)S(1)}, f32[10,24,128]{2,1,0:T(8,128)S(1)}, u32[]{:S(2)}, u32[]{:S(2)}) %collective-permute-start.2) | collective-permute-done | bytes 122912 | tf_op jit(solution)/shard_map/ppermute | solution.py:394
  22.4 4.5 %collective-permute-done.3.xb_ref = f32[10,24,128]{2,1,0:T(8,128)S(1)} collective-permute-done((f32[10,24,128]{2,1,0:T(8,128)S(1)}, f32[10,24,128]{2,1,0:T(8,128)S(1)}, u32[]{:S(2)}, u32[]{:S(2)}) %collective-permute-start.3) | collective-permute-done | bytes 122912 | tf_op jit(solution)/shard_map/ppermute | solution.py:394
  26.9 0.7 %shard_map.89 = (f32[16,24,128]{2,1,0:T(8,128)S(1)}, f32[16,24,128]{2,1,0:T(8,128)S(1)}, f32[16,24,128]{2,1,0:T(8,128)S(1)}, f32[8,16,128]{2,1,0:T(8,128)S(1)}, f32[12,24,128]{2,1,0:T(8,128)}) custom-call(f32[8,24,128]{2,1,0:T(8,128)S(1)} %get-tuple-element.38.c_ref, f32[8,24,128]{2,1,0:T(8,128)S(1)} %get-tuple-element.39.f_ref, ...), custom_call_target="tpu_custom_call" | custom-call | tf_op jit(solution)/shard_map/pallas_call | solution.py:23
  27.6 1.0 %shard_map.90 = (f32[8,16,128]{2,1,0:T(8,128)S(1)}, f32[8,4,128]{2,1,0:T(4,128)S(1)}, f32[8,4,128]{2,1,0:T(4,128)S(1)}, f32[1,128]{1,0:T(1,128)S(1)}) custom-call(s32[32]{0:T(128)S(1)} %copy-done.6, s32[1,1]{1,0:T(1,128)S(6)} %copy.11.count_ref, f32[32,1,640]{2,1,0:T(1,128)S(1)} %all-to-all-done.recv_ref.recv_w_ref, ...), custom_call_target="tpu_custom_call" | custom-call | tf_op jit(solution)/shard_map/pallas_call | solution.py:23
  28.6 2.5 %collective-permute-start.5 = (f32[8,4,128]{2,1,0:T(4,128)S(1)}, f32[8,4,128]{2,1,0:T(4,128)S(1)}, u32[]{:S(2)}, u32[]{:S(2)}) collective-permute-start(f32[8,4,128]{2,1,0:T(4,128)S(1)} %get-tuple-element.46), channel_id=1, source_target_pairs={{0,7},{1,2},{2,1},{3,4},{4,3},{5,6},{6,5},{7,0},{8,15},{9,10},{10,... | collective-permute-start | bytes 49160 | tf_op jit(solution)/shard_map/ppermute | solution.py:394
  31.1 1.6 %collective-permute-done.5.yb_ref = f32[8,4,128]{2,1,0:T(4,128)S(1)} collective-permute-done((f32[8,4,128]{2,1,0:T(4,128)S(1)}, f32[8,4,128]{2,1,0:T(4,128)S(1)}, u32[]{:S(2)}, u32[]{:S(2)}) %collective-permute-start.5) | collective-permute-done | bytes 16416 | tf_op jit(solution)/shard_map/ppermute | solution.py:394
  32.9 2.2 %collective-permute-start.7 = (f32[4,24,128]{2,1,0:T(8,128)S(1)}, f32[4,24,128]{2,1,0:T(8,128)S(1)}, u32[]{:S(2)}, u32[]{:S(2)}) collective-permute-start(f32[4,24,128]{2,1,0:T(8,128)S(1)} %get-tuple-element.49), channel_id=1, source_target_pairs={{0,24},{8,16},{16,8},{24,0},{1,25},{9,17},{17,9},{25,1},{2,26},{10... | collective-permute-start | bytes 147464 | tf_op jit(solution)/shard_map/ppermute | solution.py:394
  35.1 1.9 %collective-permute-done.6.xa_ref = f32[4,24,128]{2,1,0:T(8,128)S(1)} collective-permute-done((f32[4,24,128]{2,1,0:T(8,128)S(1)}, f32[4,24,128]{2,1,0:T(8,128)S(1)}, u32[]{:S(2)}, u32[]{:S(2)}) %collective-permute-start.6) | collective-permute-done | bytes 49184 | tf_op jit(solution)/shard_map/ppermute | solution.py:394
  36.9 2.0 %collective-permute-done.7.xb_ref = f32[4,24,128]{2,1,0:T(8,128)S(1)} collective-permute-done((f32[4,24,128]{2,1,0:T(8,128)S(1)}, f32[4,24,128]{2,1,0:T(8,128)S(1)}, u32[]{:S(2)}, u32[]{:S(2)}) %collective-permute-start.7) | collective-permute-done | bytes 49184 | tf_op jit(solution)/shard_map/ppermute | solution.py:394
  39.6 10.9 %all_to_all.15.recv_ref.recv2_ref = f32[32,1,256]{2,1,0:T(1,128)S(1)} all-to-all(f32[32,1,256]{2,1,0:T(1,128)S(1)} %get-tuple-element.54), channel_id=1, replica_groups=mesh['gx'=4,'gy'=8] {'gx','gy'}, dimensions={0} | all-to-all | bytes 65536 | tf_op jit(solution)/shard_map/all_to_all | solution.py:398
  50.5 0.9 %shard_map.93 = (f32[8,16,128]{2,1,0:T(8,128)S(1)}, f32[8,1,128]{2,1,0:T(1,128)S(1)}, f32[8,1,128]{2,1,0:T(1,128)S(1)}, f32[1,16,128]{2,1,0:T(8,128)S(1)}, f32[1,16,128]{2,1,0:T(8,128)S(1)}) custom-call(s32[32]{0:T(128)S(1)} %copy-done.6, s32[1,1]{1,0:T(1,128)S(6)} %copy.11.count_ref, f32[32,1,256]{2,1,0:T(1,128)S(1)} %all_to_all.15.recv_ref.recv2_ref, ...), custom_call_target="tpu_custom_call" | custom-call | tf_op jit(solution)/shard_map/pallas_call | solution.py:23
  52.0 1.5 %collective-permute-start.11 = (f32[1,16,128]{2,1,0:T(8,128)S(1)}, f32[1,16,128]{2,1,0:T(8,128)S(1)}, u32[]{:S(2)}, u32[]{:S(2)}) collective-permute-start(f32[1,16,128]{2,1,0:T(8,128)S(1)} %get-tuple-element.59), channel_id=1, source_target_pairs={{0,24},{8,16},{16,8},{24,0},{1,25},{9,17},{17,9},{25,1},{2,26},{10... | collective-permute-start | bytes 24584 | tf_op jit(solution)/shard_map/ppermute | solution.py:394
  54.7 2.8 %collective-permute-done.9.yb_ref = f32[8,1,128]{2,1,0:T(1,128)S(1)} collective-permute-done((f32[8,1,128]{2,1,0:T(1,128)S(1)}, f32[8,1,128]{2,1,0:T(1,128)S(1)}, u32[]{:S(2)}, u32[]{:S(2)}) %collective-permute-start.9) | collective-permute-done | bytes 4128 | tf_op jit(solution)/shard_map/ppermute | solution.py:394
  57.7 9.9 %all_to_all.16.recv3_ref = f32[32,1,128]{2,1,0:T(1,128)S(1)} all-to-all(f32[32,1,128]{2,1,0:T(1,128)S(1)} %get-tuple-element.63), channel_id=1, replica_groups=mesh['gx'=4,'gy'=8] {'gx','gy'}, dimensions={0} | all-to-all | bytes 32768 | tf_op jit(solution)/shard_map/all_to_all | solution.py:398
  67.6 1.1 %shard_map.95 = (f32[8,16,128]{2,1,0:T(8,128)}, f32[8,16,128]{2,1,0:T(8,128)}) custom-call(f32[32,1,256]{2,1,0:T(1,128)S(1)} %all_to_all.15.recv_ref.recv2_ref, f32[32,1,128]{2,1,0:T(1,128)S(1)} %all_to_all.16.recv3_ref, f32[8,16,128]{2,1,0:T(8,128)S(1)} %copy-done.3, f32[8,16,128]{2,1,0:T(8,128)S(1)} %get-tuple-element.44.d_ref, ...), custom_call_target="tpu_custom_call" | custom-call | tf_op jit(solution)/shard_map/pallas_call | solution.py:23
  (32 shorter events, 4.4 us)
Async XLA Ops:
  0.6 0.8 %copy-start.2 = (f32[8,16,128]{2,1,0:T(8,128)S(1)}, f32[8,16,128]{2,1,0:T(8,128)}, u32[]{:S(2)}) copy-start(f32[8,16,128]{2,1,0:T(8,128)} %rhs_ref.11) | copy-start | bytes 196612
  1.5 0.8 %copy-start.4 = (f32[8,16,128]{2,1,0:T(8,128)S(1)}, f32[8,16,128]{2,1,0:T(8,128)}, u32[]{:S(2)}) copy-start(f32[8,16,128]{2,1,0:T(8,128)} %diag_ref.1) | copy-start | bytes 196612
  2.3 0.8 %copy-start.5 = (s32[8,16,128]{2,1,0:T(8,128)S(1)}, s32[8,16,128]{2,1,0:T(8,128)}, u32[]{:S(2)}) copy-start(s32[8,16,128]{2,1,0:T(8,128)} %solid_ref.1) | copy-start | bytes 196612
  3.2 4.8 %copy-start.7 = (f32[128,64]{0,1:T(8,128)S(1)}, f32[128,64]{0,1:T(8,128)}, u32[]{:S(2)}) copy-start(f32[128,64]{0,1:T(8,128)} %param.13) | copy-start | bytes 98308
  3.2 12.4 %collective-permute-start = (f32[24,4,128]{2,1,0:T(4,128)S(1)}, f32[24,4,128]{2,1,0:T(4,128)S(1)}, u32[]{:S(2)}, u32[]{:S(2)}) collective-permute-start(f32[24,4,128]{2,1,0:T(4,128)S(1)} %get-tuple-element.36), channel_id=1, source_target_pairs={{0,1},{1,0},{2,3},{3,2},{4,5},{5,4},{6,7},{7,6},{8,9},{9,8},{10,11... | collective-permute-start | bytes 147464 | tf_op jit(solution)/shard_map/ppermute | solution.py:394
  3.7 11.9 %collective-permute-start.1 = (f32[24,4,128]{2,1,0:T(4,128)S(1)}, f32[24,4,128]{2,1,0:T(4,128)S(1)}, u32[]{:S(2)}, u32[]{:S(2)}) collective-permute-start(f32[24,4,128]{2,1,0:T(4,128)S(1)} %get-tuple-element.37), channel_id=1, source_target_pairs={{0,7},{1,2},{2,1},{3,4},{4,3},{5,6},{6,5},{7,0},{8,15},{9,10},{10,... | collective-permute-start | bytes 147464 | tf_op jit(solution)/shard_map/ppermute | solution.py:394
  8.1 0.8 %copy-start.3 = (f32[8,16,128]{2,1,0:T(8,128)S(1)}, f32[8,16,128]{2,1,0:T(8,128)}, u32[]{:S(2)}) copy-start(f32[8,16,128]{2,1,0:T(8,128)} %rhs_ref.11) | copy-start | bytes 196612
  8.1 0.8 %copy-start.6 = (s32[32]{0:T(128)S(1)}, s32[32]{0:T(128)}, u32[]{:S(2)}) copy-start(s32[32]{0:T(128)} %slots_ref.5) | copy-start | bytes 388
  8.9 1.2 %copy-start = (bf16[32,8,16,128]{3,2,1,0:T(8,128)(2,1)S(1)}, bf16[32,8,16,128]{3,2,1,0:T(8,128)(2,1)}, u32[]{:S(2)}) copy-start(bf16[32,8,16,128]{3,2,1,0:T(8,128)(2,1)} %vec_ref.7) | copy-start | bytes 3145732
  10.1 17.5 %copy-start.1 = (bf16[32,8,16,128]{3,2,1,0:T(8,128)(2,1)S(1)}, bf16[32,8,16,128]{3,2,1,0:T(8,128)(2,1)}, u32[]{:S(2)}) copy-start(bf16[32,8,16,128]{3,2,1,0:T(8,128)(2,1)} %vec_ref.7) | copy-start | bytes 3145732
  11.6 16.0 %all-to-all-start = ((f32[32,1,640]{2,1,0:T(1,128)}), f32[32,1,640]{2,1,0:T(1,128)S(1)}, u32[]{:S(2)}, u32[]{:S(2)}) async-start(f32[32,1,640]{2,1,0:T(1,128)} %shard_map.86), calls=%async_computation | async-start | bytes 163840 | tf_op jit(solution)/shard_map/all_to_all | solution.py:398
  15.7 6.7 %collective-permute-start.2 = (f32[10,24,128]{2,1,0:T(8,128)S(1)}, f32[10,24,128]{2,1,0:T(8,128)S(1)}, u32[]{:S(2)}, u32[]{:S(2)}) collective-permute-start(f32[10,24,128]{2,1,0:T(8,128)S(1)} %get-tuple-element.41), channel_id=1, source_target_pairs={{0,8},{8,0},{16,24},{24,16},{1,9},{9,1},{17,25},{25,17},{2,10},{10... | collective-permute-start | bytes 368648 | tf_op jit(solution)/shard_map/ppermute | solution.py:394
  17.5 9.3 %collective-permute-start.3 = (f32[10,24,128]{2,1,0:T(8,128)S(1)}, f32[10,24,128]{2,1,0:T(8,128)S(1)}, u32[]{:S(2)}, u32[]{:S(2)}) collective-permute-start(f32[10,24,128]{2,1,0:T(8,128)S(1)} %get-tuple-element.42), channel_id=1, source_target_pairs={{0,24},{8,16},{16,8},{24,0},{1,25},{9,17},{17,9},{25,1},{2,26},{10... | collective-permute-start | bytes 368648 | tf_op jit(solution)/shard_map/ppermute | solution.py:394
  28.6 2.5 %collective-permute-start.4 = (f32[8,4,128]{2,1,0:T(4,128)S(1)}, f32[8,4,128]{2,1,0:T(4,128)S(1)}, u32[]{:S(2)}, u32[]{:S(2)}) collective-permute-start(f32[8,4,128]{2,1,0:T(4,128)S(1)} %get-tuple-element.45), channel_id=1, source_target_pairs={{0,1},{1,0},{2,3},{3,2},{4,5},{5,4},{6,7},{7,6},{8,9},{9,8},{10,11... | collective-permute-start | bytes 49160 | tf_op jit(solution)/shard_map/ppermute | solution.py:394
  28.6 4.1 %collective-permute-start.5 = (f32[8,4,128]{2,1,0:T(4,128)S(1)}, f32[8,4,128]{2,1,0:T(4,128)S(1)}, u32[]{:S(2)}, u32[]{:S(2)}) collective-permute-start(f32[8,4,128]{2,1,0:T(4,128)S(1)} %get-tuple-element.46), channel_id=1, source_target_pairs={{0,7},{1,2},{2,1},{3,4},{4,3},{5,6},{6,5},{7,0},{8,15},{9,10},{10,... | collective-permute-start | bytes 49160 | tf_op jit(solution)/shard_map/ppermute | solution.py:394
  32.8 4.2 %collective-permute-start.6 = (f32[4,24,128]{2,1,0:T(8,128)S(1)}, f32[4,24,128]{2,1,0:T(8,128)S(1)}, u32[]{:S(2)}, u32[]{:S(2)}) collective-permute-start(f32[4,24,128]{2,1,0:T(8,128)S(1)} %get-tuple-element.48), channel_id=1, source_target_pairs={{0,8},{8,0},{16,24},{24,16},{1,9},{9,1},{17,25},{25,17},{2,10},{10... | collective-permute-start | bytes 147464 | tf_op jit(solution)/shard_map/ppermute | solution.py:394
  32.9 6.1 %collective-permute-start.7 = (f32[4,24,128]{2,1,0:T(8,128)S(1)}, f32[4,24,128]{2,1,0:T(8,128)S(1)}, u32[]{:S(2)}, u32[]{:S(2)}) collective-permute-start(f32[4,24,128]{2,1,0:T(8,128)S(1)} %get-tuple-element.49), channel_id=1, source_target_pairs={{0,24},{8,16},{16,8},{24,0},{1,25},{9,17},{17,9},{25,1},{2,26},{10... | collective-permute-start | bytes 147464 | tf_op jit(solution)/shard_map/ppermute | solution.py:394
  51.4 6.1 %collective-permute-start.10 = (f32[1,16,128]{2,1,0:T(8,128)S(1)}, f32[1,16,128]{2,1,0:T(8,128)S(1)}, u32[]{:S(2)}, u32[]{:S(2)}) collective-permute-start(f32[1,16,128]{2,1,0:T(8,128)S(1)} %get-tuple-element.58), channel_id=1, source_target_pairs={{0,8},{8,0},{16,24},{24,16},{1,9},{9,1},{17,25},{25,17},{2,10},{10... | collective-permute-start | bytes 24584 | tf_op jit(solution)/shard_map/ppermute | solution.py:394
  52.0 5.4 %collective-permute-start.11 = (f32[1,16,128]{2,1,0:T(8,128)S(1)}, f32[1,16,128]{2,1,0:T(8,128)S(1)}, u32[]{:S(2)}, u32[]{:S(2)}) collective-permute-start(f32[1,16,128]{2,1,0:T(8,128)S(1)} %get-tuple-element.59), channel_id=1, source_target_pairs={{0,24},{8,16},{16,8},{24,0},{1,25},{9,17},{17,9},{25,1},{2,26},{10... | collective-permute-start | bytes 24584 | tf_op jit(solution)/shard_map/ppermute | solution.py:394
  53.5 1.2 %collective-permute-start.8 = (f32[8,1,128]{2,1,0:T(1,128)S(1)}, f32[8,1,128]{2,1,0:T(1,128)S(1)}, u32[]{:S(2)}, u32[]{:S(2)}) collective-permute-start(f32[8,1,128]{2,1,0:T(1,128)S(1)} %get-tuple-element.56), channel_id=1, source_target_pairs={{0,1},{1,0},{2,3},{3,2},{4,5},{5,4},{6,7},{7,6},{8,9},{9,8},{10,11... | collective-permute-start | bytes 12296 | tf_op jit(solution)/shard_map/ppermute | solution.py:394
  53.5 3.9 %collective-permute-start.9 = (f32[8,1,128]{2,1,0:T(1,128)S(1)}, f32[8,1,128]{2,1,0:T(1,128)S(1)}, u32[]{:S(2)}, u32[]{:S(2)}) collective-permute-start(f32[8,1,128]{2,1,0:T(1,128)S(1)} %get-tuple-element.57), channel_id=1, source_target_pairs={{0,7},{1,2},{2,1},{3,4},{4,3},{5,6},{6,5},{7,0},{8,15},{9,10},{10,... | collective-permute-start | bytes 12296 | tf_op jit(solution)/shard_map/ppermute | solution.py:394
